TPU v7x, 32 devices: a whole 2x2x4 slice. The times are simulated.
32 devices in a mesh: band: 2 (over x), grid: 16 (over z, y, core).
Axes of the slice: x: 2, y: 2, z: 4, core: 2. Of those that a mesh axis runs over, the one named last changes fastest.
Arguments:
- start_block: float32 [64, 128, 4, 128], P('band', 'grid'), may hold values from -6 to 6
- previous_block: float32 [64, 128, 4, 128], P('band', 'grid'), may hold values from -6 to 6
- previous_coupling: float32 [64, 64], replicated, may hold values from -0.75 to 0.75
- potential: float32 [128, 4, 128], P('grid'), may hold values from -2 to 2
- atom_cells: int32 [128, 128], P('grid'), may hold values from 0 to 7167, as said below
- atom_proj: float32 [128, 4, 128], P('grid'), may hold values from -1.08 to 1.08
- atom_strength: float32 [128, 4], P('grid'), may hold values from 0.5 to 4
- atom_count: int32 [16], P('grid'), may hold values from 1 to 8, as said below
Outputs:
- a_blocks: float32 [2, 64, 64], P(None, None, 'band')
- b_blocks: float32 [2, 64, 64], P(None, None, 'band')
- final_block: float32 [64, 128, 4, 128], P('band', 'grid')
Inputs may be any that keep to these rules, and one draw needn't show every extreme that they name: `atom_cells`: row a lists 128 distinct cells of atom a's sphere as row-major indices over (14) planes x 4 x 128, counted from the first plane of the slab that holds row a; indices of 4096 or more lie in the first 6 planes of the next slab; on the last slab every index is below 4096. `atom_count`: slots at or past a slab's count are not atoms.
All inputs are finite; a program needn't handle non-finite values.
Results may differ from a plain program's by a relative error of at most 0.0003.
Values sent between devices are 32-bit elements; how exact they have to be, the bound alone decides.
A program may use at most 64 MiB of HBM per device.

v0:
```python
import jax
import jax.numpy as jnp
from jax import lax
from jax.sharding import PartitionSpec as P

NB = 64
STEPS = 2


HIGHEST = lax.Precision.HIGHEST
STENCIL_WEIGHTS = (
    -5369.0 / 1800.0,
    12.0 / 7.0,
    -15.0 / 56.0,
    10.0 / 189.0,
    -1.0 / 112.0,
    2.0 / 1925.0,
    -1.0 / 16632.0,
)


def extended_2(block, sides, width):
    for axis, dim in sides:
        count = lax.axis_size(axis)
        forward = [(i, i + 1) for i in range(count - 1)]
        backward = [(target, source) for source, target in forward]
        low = lax.ppermute(
            lax.slice_in_dim(block, block.shape[dim] - width, None, axis=dim), axis, forward
        )
        high = lax.ppermute(lax.slice_in_dim(block, 0, width, axis=dim), axis, backward)
        block = jnp.concatenate([low, block, high], axis=dim)
    return block


def from_behind(block, axis, distance):
    devices = range(lax.axis_size(axis))
    route = [(i - distance, i) for i in devices if i - distance in devices]
    return lax.ppermute(block, axis, route)


def kinetic_local(haloed, planes):
    center = haloed[:, 6 : 6 + planes]
    width_y, width_z = (center.shape[2], center.shape[3])
    padded = jnp.pad(center, ((0, 0), (0, 0), (6, 6), (6, 6)))
    laplace = 3.0 * STENCIL_WEIGHTS[0] * center
    for k in range(1, 7):
        laplace = laplace + STENCIL_WEIGHTS[k] * (
            haloed[:, 6 + k : 6 + k + planes] + haloed[:, 6 - k : 6 - k + planes]
        )
        laplace = laplace + STENCIL_WEIGHTS[k] * (
            padded[:, :, 6 + k : 6 + k + width_y, 6 : 6 + width_z]
            + padded[:, :, 6 - k : 6 - k + width_y, 6 : 6 + width_z]
        )
        laplace = laplace + STENCIL_WEIGHTS[k] * (
            padded[:, :, 6 : 6 + width_y, 6 + k : 6 + k + width_z]
            + padded[:, :, 6 : 6 + width_y, 6 - k : 6 - k + width_z]
        )
    return -0.5 * laplace


def projector_terms(extended, atom_cells, atom_proj, atom_strength, live_count):
    states_dev = extended.shape[0]
    atom_slots, points = atom_cells.shape
    cell_list = atom_cells.reshape(-1)
    picked = jnp.take(extended, cell_list, axis=1).reshape(states_dev, atom_slots, points)
    coefficient = jnp.einsum("sap,ajp->saj", picked, atom_proj, precision=HIGHEST)
    live_mask = (jnp.arange(atom_slots, dtype=jnp.int32) < live_count).astype(jnp.float32)
    scaled = coefficient * (atom_strength * live_mask[:, None])[None]
    spread = jnp.einsum("saj,ajp->sap", scaled, atom_proj, precision=HIGHEST)
    return jnp.zeros_like(extended).at[:, cell_list].add(spread.reshape(states_dev, -1))


def factor_of(gram):
    factor = jnp.linalg.cholesky(gram)
    identity = jnp.eye(gram.shape[0], dtype=jnp.float32)
    inverse = jax.scipy.linalg.solve_triangular(factor, identity, lower=True)
    return (factor, inverse)


def shards(
    start_block,
    previous_block,
    previous_coupling,
    potential,
    atom_cells,
    atom_proj,
    atom_strength,
    atom_count,
):
    states_dev, planes, width_y, width_z = start_block.shape
    cell_total = planes * lax.axis_size("grid") * width_y * width_z
    offset = lax.axis_index("band") * states_dev
    live_count = atom_count[0]
    a_list = []
    b_list = []

    def to_cells(block):
        return lax.all_to_all(block, "band", split_axis=1, concat_axis=0, tiled=True)

    def to_states(block):
        return lax.all_to_all(block, "band", split_axis=0, concat_axis=1, tiled=True)

    def summed(matrix):
        return lax.psum(matrix, ("band", "grid"))

    start_cells = to_cells(start_block)
    cell_shape = start_cells.shape
    start_flat = start_cells.reshape(NB, -1)
    factor, inverse = factor_of(
        summed(jnp.dot(start_flat, start_flat.T, precision=HIGHEST) / cell_total)
    )
    current_cells = jnp.dot(inverse, start_flat, precision=HIGHEST)
    previous_cells = to_cells(previous_block).reshape(NB, -1)
    coupling = previous_coupling
    current_local = to_states(current_cells.reshape(cell_shape))
    for iteration in range(STEPS):
        haloed = extended_2(current_local, (("grid", 1),), 6)
        kinetic_part = kinetic_local(haloed, planes)
        extended = haloed[:, 6:].reshape(states_dev, -1)
        terms = projector_terms(extended, atom_cells, atom_proj, atom_strength, live_count)
        terms = terms.reshape(states_dev, planes + 6, width_y, width_z)
        received = from_behind(terms[:, planes:], "grid", 1)
        own_terms = terms[:, :planes].at[:, :6].add(received)
        applied = kinetic_part + potential[None] * current_local + own_terms
        applied_cells = to_cells(applied).reshape(NB, -1)
        correlation = summed(
            jnp.dot(current_cells, applied_cells.T, precision=HIGHEST) / cell_total
        )
        residual_block = (
            applied_cells
            - jnp.dot(correlation.T, current_cells, precision=HIGHEST)
            - jnp.dot(coupling, previous_cells, precision=HIGHEST)
        )
        factor, inverse = factor_of(
            summed(jnp.dot(residual_block, residual_block.T, precision=HIGHEST) / cell_total)
        )
        coupling = factor.T
        a_list.append(lax.dynamic_slice_in_dim(correlation, offset, states_dev, 1))
        b_list.append(lax.dynamic_slice_in_dim(coupling, offset, states_dev, 1))
        previous_cells = current_cells
        current_cells = jnp.dot(inverse, residual_block, precision=HIGHEST)
        current_local = to_states(current_cells.reshape(cell_shape))
    return (jnp.stack(a_list), jnp.stack(b_list), current_local)


def solution(mesh):
    in_specs = (
        P("band", "grid", None, None),
        P("band", "grid", None, None),
        P(),
        P("grid", None, None),
        P("grid", None),
        P("grid", None, None),
        P("grid", None),
        P("grid"),
    )
    out_specs = (P(None, None, "band"), P(None, None, "band"), P("band", "grid", None, None))
    return jax.shard_map(shards, mesh=mesh, in_specs=in_specs, out_specs=out_specs, check_vma=False)
```

profile of v0, /device:TPU:0, one launch (start us, length us, event | category | flops | bytes accessed | tf_op | source)
XLA Modules:
  0.0 424.2 jit_solution(2157985983389813124)
XLA Ops:
  0.6 1.9 copy.51
  2.6 4.3 %all-to-all-start = ((f32[32,8,4,128]{3,2,0,1:T(4,128)}), f32[32,8,4,128]{3,2,0,1:T(4,128)S(1)}, u32[]{:S(2)}, u32[]{:S(2)}) async-start(f32[32,8,4,128]{3,2,0,1:T(4,128)} %copy.51), calls=%async_computation | async-start | bytes 1048576 | tf_op jit(solution)/shard_map/all_to_all | solution.py:98
  7.6 8.1 %all-to-all-done = f32[32,8,4,128]{3,2,0,1:T(4,128)S(1)} async-done(((f32[32,8,4,128]{3,2,0,1:T(4,128)}), f32[32,8,4,128]{3,2,0,1:T(4,128)S(1)}, u32[]{:S(2)}, u32[]{:S(2)}) %all-to-all-start) | async-done | bytes 524320 | tf_op jit(solution)/shard_map/all_to_all | solution.py:98
  16.5 40.0 %psum.35 = f32[64,64]{0,1:T(8,128)S(1)} all-reduce(f32[64,64]{0,1:T(8,128)S(1)} %convolution_multiply_fusion.4), channel_id=1, replica_groups=mesh['band'=2,'grid'=16] {'band','grid'}, use_global_device_ids=true, to_apply=%region_0.0 | all-reduce | flops 4096 | bytes 32768 | tf_op jit(solution)/shard_map/psum | solution.py:104
  56.6 5.8 %cholesky.59 = f32[64,64]{1,0:T(8,128)S(1)} custom-call(f32[64,64]{1,0:T(8,128)S(1)} %fusion.140), custom_call_target="Cholesky" | custom-call | tf_op jit(solution)/shard_map/jit(cholesky)/cholesky | solution.py:74
  63.8 4.9 %custom-call.7 = f32[1,64,64]{1,2,0:T(8,128)S(1)} custom-call(f32[1,64,64]{2,1,0:T(8,128)S(1)} %fusion.134), custom_call_target="InvertDiagBlocksLowerTriangular" | custom-call | tf_op jit(solution)/shard_map/jit(_solve_triangular)/triangular_solve | solution.py:76
  70.7 3.5 all-to-all-start.1
  74.3 7.9 %all-to-all-done.1 = f32[64,4,4,128]{3,2,1,0:T(4,128)S(1)} async-done(((f32[64,4,4,128]{3,2,1,0:T(4,128)}), f32[64,4,4,128]{3,2,1,0:T(4,128)S(1)}, u32[]{:S(2)}, u32[]{:S(2)}) %all-to-all-start.1) | async-done | bytes 524320 | tf_op jit(solution)/shard_map/all_to_all | solution.py:101
  84.5 2.3 collective-permute-done
  87.6 2.4 copy.56
  90.1 4.8 %gather_fusion = f32[1024,32]{1,0:T(8,128)S(1)} fusion(f32[32,7168]{0,1:T(8,128)} %bitcast.150, s32[1024]{0:T(1024)S(1)} %fusion.141), kind=kCustom, calls=%fused_computation.clone | custom fusion | bytes 266240 | tf_op jit(solution)/shard_map/jit(_take)/gather | solution.py:65
  96.3 8.0 %scatter_custom_fusion = f32[32,7168]{0,1:T(8,128)} fusion(s32[1024]{0:T(1024)S(1)} %bitcast.165, f32[1024,32]{1,0:T(8,128)S(1)} %copy.60, f32[]{:T(128)} %constant.127.clone.1), kind=kCustom, calls=%fused_computation.60 | custom fusion | flops 32768 | bytes 917508 | tf_op jit(solution)/shard_map/scatter-add | solution.py:70
  104.3 3.4 fusion.143
  108.9 8.3 %collective-permute-start.2 = (f32[32,6,4,128]{3,0,2,1:T(8,128)}, f32[32,6,4,128]{3,0,2,1:T(8,128)}, u32[]{:S(2)}, u32[]{:S(2)}) collective-permute-start(f32[32,6,4,128]{3,0,2,1:T(8,128)} %copy.92), channel_id=1, source_target_pairs={{0,1},{1,2},{2,3},{3,4},{4,5},{5,6},{6,7},{7,8},{8,9},{9,10},{10,1... | collective-permute-start | bytes 1179656 | tf_op jit(solution)/shard_map/ppermute | solution.py:38
  117.2 2.0 collective-permute-start.1
  120.2 4.2 all-to-all-start.3
  124.4 1.7 slice.410
  126.1 2.6 copy.91
  128.7 1.4 copy.90
  130.1 1.9 add_dynamic-update-slice_fusion.1
  132.0 4.3 %fusion.51 = f32[32,8,4,128]{3,0,2,1:T(8,128)} fusion(f32[32,8,4,128]{3,0,2,1:T(8,128)} %add_dynamic-update-slice_fusion.1, f32[32,8,4,128]{3,0,2,1:T(8,128)S(1)} %bitcast.145, f32[32,6,4,128]{3,0,2,1:T(8,128)} %collective-permute-done.1, f32[32,6,4,128]{3,0,2,1:T(8,128)} %copy-done.3, f32[8,4,128]{2,1,0:T(4,128)S(1)} %copy-done.7), kind=kLoop, calls=%fused_computation.150 | loop fusion | flops 8388608 | bytes 2375680 | tf_op jit(solution)/shard_map/add | solution.py:124
  136.4 3.7 all-to-all-start.2
  141.4 7.5 %all-to-all-done.2 = f32[32,8,4,128]{3,0,2,1:T(8,128)S(1)} async-done(((f32[32,8,4,128]{3,0,2,1:T(8,128)}), f32[32,8,4,128]{3,0,2,1:T(8,128)S(1)}, u32[]{:S(2)}, u32[]{:S(2)}) %all-to-all-start.2) | async-done | bytes 524320 | tf_op jit(solution)/shard_map/all_to_all | solution.py:98
  150.0 38.9 %psum.36 = f32[64,64]{0,1:T(8,128)S(1)} all-reduce(f32[64,64]{0,1:T(8,128)S(1)} %convolution_multiply_fusion.3), channel_id=1, replica_groups=mesh['band'=2,'grid'=16] {'band','grid'}, use_global_device_ids=true, to_apply=%region_4.8 | all-reduce | flops 4096 | bytes 32768 | tf_op jit(solution)/shard_map/psum | solution.py:104
  190.7 39.4 %psum.37 = f32[64,64]{0,1:T(8,128)S(1)} all-reduce(f32[64,64]{0,1:T(8,128)S(1)} %convolution_multiply_fusion.2), channel_id=1, replica_groups=mesh['band'=2,'grid'=16] {'band','grid'}, use_global_device_ids=true, to_apply=%region_5.9 | all-reduce | flops 4096 | bytes 32768 | tf_op jit(solution)/shard_map/psum | solution.py:104
  230.2 5.8 %cholesky.70 = f32[64,64]{1,0:T(8,128)S(1)} custom-call(f32[64,64]{1,0:T(8,128)S(1)} %fusion.138), custom_call_target="Cholesky" | custom-call | tf_op jit(solution)/shard_map/jit(cholesky)/cholesky | solution.py:74
  237.4 4.9 %custom-call.8 = f32[1,64,64]{1,2,0:T(8,128)S(1)} custom-call(f32[1,64,64]{2,1,0:T(8,128)S(1)} %get-tuple-element.32), custom_call_target="InvertDiagBlocksLowerTriangular" | custom-call | tf_op jit(solution)/shard_map/jit(_solve_triangular)/triangular_solve | solution.py:76
  243.5 10.8 %all_to_all.114 = f32[64,4,4,128]{3,2,1,0:T(4,128)S(1)} all-to-all(f32[64,4,4,128]{3,2,1,0:T(4,128)S(1)} %reshape.189), channel_id=1, replica_groups=mesh['band'=2,'grid'=16] {'band'}, dimensions={0} | all-to-all | bytes 1048576 | tf_op jit(solution)/shard_map/all_to_all | solution.py:101
  256.6 2.3 collective-permute-done.3
  259.7 2.4 copy.71
  262.1 4.8 %gather_fusion.1 = f32[1024,32]{1,0:T(8,128)S(1)} fusion(f32[32,7168]{0,1:T(8,128)} %bitcast.149, s32[1024]{0:T(1024)S(1)} %fusion.141), kind=kCustom, calls=%fused_computation.1.clone | custom fusion | bytes 266240 | tf_op jit(solution)/shard_map/jit(_take)/gather | solution.py:65
  268.4 8.0 %scatter_custom_fusion.1 = f32[32,7168]{0,1:T(8,128)} fusion(s32[1024]{0:T(1024)S(1)} %bitcast.166, f32[1024,32]{1,0:T(8,128)S(1)} %copy.74, f32[]{:T(128)} %constant.127.clone.1), kind=kCustom, calls=%fused_computation.58 | custom fusion | flops 32768 | bytes 917508 | tf_op jit(solution)/shard_map/scatter-add | solution.py:70
  276.4 3.3 fusion.142
  280.9 8.4 %collective-permute-start.5 = (f32[32,6,4,128]{3,0,2,1:T(8,128)}, f32[32,6,4,128]{3,0,2,1:T(8,128)}, u32[]{:S(2)}, u32[]{:S(2)}) collective-permute-start(f32[32,6,4,128]{3,0,2,1:T(8,128)} %copy.95), channel_id=1, source_target_pairs={{0,1},{1,2},{2,3},{3,4},{4,5},{5,6},{6,7},{7,8},{8,9},{9,10},{10,1... | collective-permute-start | bytes 1179656 | tf_op jit(solution)/shard_map/ppermute | solution.py:38
  289.3 2.0 collective-permute-start.4
  291.4 1.7 slice.437
  293.1 2.6 copy.94
  295.7 1.4 copy.93
  297.1 2.0 add_dynamic-update-slice_fusion
  299.0 4.5 %fusion.16 = f32[32,8,4,128]{3,0,2,1:T(8,128)} fusion(f32[32,8,4,128]{3,0,2,1:T(8,128)} %add_dynamic-update-slice_fusion, f32[32,8,4,128]{3,0,2,1:T(8,128)S(1)} %bitcast.148, f32[32,6,4,128]{3,0,2,1:T(8,128)} %collective-permute-done.4, f32[32,6,4,128]{3,0,2,1:T(8,128)} %copy-done.4, f32[8,4,128]{2,1,0:T(4,128)S(1)} %copy-done.7), kind=kLoop, calls=%fused_computation.115 | loop fusion | flops 8388608 | bytes 2375680 | tf_op jit(solution)/shard_map/add | solution.py:124
  303.6 3.5 all-to-all-start.5
  307.1 8.5 %all-to-all-done.5 = f32[32,8,4,128]{3,0,2,1:T(8,128)S(1)} async-done(((f32[32,8,4,128]{3,0,2,1:T(8,128)}), f32[32,8,4,128]{3,0,2,1:T(8,128)S(1)}, u32[]{:S(2)}, u32[]{:S(2)}) %all-to-all-start.5) | async-done | bytes 524320 | tf_op jit(solution)/shard_map/all_to_all | solution.py:98
  316.7 39.2 %psum.38 = f32[64,64]{0,1:T(8,128)S(1)} all-reduce(f32[64,64]{0,1:T(8,128)S(1)} %convolution_multiply_fusion.1), channel_id=1, replica_groups=mesh['band'=2,'grid'=16] {'band','grid'}, use_global_device_ids=true, to_apply=%region_7.11 | all-reduce | flops 4096 | bytes 32768 | tf_op jit(solution)/shard_map/psum | solution.py:104
  357.8 40.5 %psum.39 = f32[64,64]{0,1:T(8,128)S(1)} all-reduce(f32[64,64]{0,1:T(8,128)S(1)} %convolution_multiply_fusion), channel_id=1, replica_groups=mesh['band'=2,'grid'=16] {'band','grid'}, use_global_device_ids=true, to_apply=%region_8.12 | all-reduce | flops 4096 | bytes 32768 | tf_op jit(solution)/shard_map/psum | solution.py:104
  398.3 5.8 %cholesky.81 = f32[64,64]{1,0:T(8,128)S(1)} custom-call(f32[64,64]{1,0:T(8,128)S(1)} %fusion.136), custom_call_target="Cholesky" | custom-call | tf_op jit(solution)/shard_map/jit(cholesky)/cholesky | solution.py:74
  405.5 4.9 %custom-call.9 = f32[1,64,64]{1,2,0:T(8,128)S(1)} custom-call(f32[1,64,64]{2,1,0:T(8,128)S(1)} %get-tuple-element.30), custom_call_target="InvertDiagBlocksLowerTriangular" | custom-call | tf_op jit(solution)/shard_map/jit(_solve_triangular)/triangular_solve | solution.py:76
  412.4 3.5 all-to-all-start.6
  417.2 6.2 %all-to-all-done.6 = f32[64,4,4,128]{3,2,1,0:T(4,128)S(1)} async-done(((f32[64,4,4,128]{3,2,1,0:T(4,128)}), f32[64,4,4,128]{3,2,1,0:T(4,128)S(1)}, u32[]{:S(2)}, u32[]{:S(2)}) %all-to-all-start.6) | async-done | bytes 524320 | tf_op jit(solution)/shard_map/all_to_all | solution.py:101
  (100 shorter events, 31.8 us)
Async XLA Ops:
  0.6 188.9 %copy-start = (f32[64,64]{1,0:T(8,128)S(1)}, f32[64,64]{1,0:T(8,128)}, u32[]{:S(2)}) copy-start(f32[64,64]{1,0:T(8,128)} %param.19) | copy-start | bytes 49156
  2.6 71.6 %copy-start.9 = (f32[8,4]{0,1:T(4,128)S(1)}, f32[8,4]{0,1:T(4,128)}, u32[]{:S(2)}) copy-start(f32[8,4]{0,1:T(4,128)} %param.23) | copy-start | bytes 388
  2.6 71.7 %copy-start.8 = (s32[8,128]{1,0:T(8,128)S(1)}, s32[8,128]{1,0:T(8,128)}, u32[]{:S(2)}) copy-start(s32[8,128]{1,0:T(8,128)} %param.21) | copy-start | bytes 12292
  2.6 13.1 %all-to-all-start = ((f32[32,8,4,128]{3,2,0,1:T(4,128)}), f32[32,8,4,128]{3,2,0,1:T(4,128)S(1)}, u32[]{:S(2)}, u32[]{:S(2)}) async-start(f32[32,8,4,128]{3,2,0,1:T(4,128)} %copy.51), calls=%async_computation | async-start | bytes 1048576 | tf_op jit(solution)/shard_map/all_to_all | solution.py:98
  70.7 11.5 %all-to-all-start.1 = ((f32[64,4,4,128]{3,2,1,0:T(4,128)}), f32[64,4,4,128]{3,2,1,0:T(4,128)S(1)}, u32[]{:S(2)}, u32[]{:S(2)}) async-start(f32[64,4,4,128]{3,2,1,0:T(4,128)} %reshape.180), calls=%async_computation.1 | async-start | bytes 1048576 | tf_op jit(solution)/shard_map/all_to_all | solution.py:101
  83.2 3.6 collective-permute-start
  86.8 0.8 copy-start.3
  87.6 7.5 %copy-start.6 = (f32[8,4,128]{2,1,0:T(4,128)S(1)}, f32[8,4,128]{2,1,0:T(4,128)}, u32[]{:S(2)}) copy-start(f32[8,4,128]{2,1,0:T(4,128)} %param.22) | copy-start | bytes 49156
  104.3 14.9 %copy-start.5 = (f32[32,8,4,128]{3,2,1,0:T(4,128)S(1)}, f32[32,8,4,128]{3,2,1,0:T(4,128)}, u32[]{:S(2)}) copy-start(f32[32,8,4,128]{3,2,1,0:T(4,128)} %param.18) | copy-start | bytes 1572868
  108.9 21.2 %collective-permute-start.2 = (f32[32,6,4,128]{3,0,2,1:T(8,128)}, f32[32,6,4,128]{3,0,2,1:T(8,128)}, u32[]{:S(2)}, u32[]{:S(2)}) collective-permute-start(f32[32,6,4,128]{3,0,2,1:T(8,128)} %copy.92), channel_id=1, source_target_pairs={{0,1},{1,2},{2,3},{3,4},{4,5},{5,6},{6,7},{7,8},{8,9},{9,10},{10,1... | collective-permute-start | bytes 1179656 | tf_op jit(solution)/shard_map/ppermute | solution.py:38
  117.2 14.8 %collective-permute-start.1 = (f32[32,6,4,128]{3,0,2,1:T(8,128)}, f32[32,6,4,128]{3,0,2,1:T(8,128)}, u32[]{:S(2)}, u32[]{:S(2)}) collective-permute-start(f32[32,6,4,128]{3,0,2,1:T(8,128)} %get-tuple-element.40), channel_id=1, source_target_pairs={{0,1},{1,2},{2,3},{3,4},{4,5},{5,6},{6,7},{7,8},{8,9},{9,10},{10,1... | collective-permute-start | bytes 1179656 | tf_op jit(solution)/shard_map/ppermute | solution.py:27
  120.2 16.2 %all-to-all-start.3 = ((f32[32,8,4,128]{3,2,0,1:T(4,128)}), f32[32,8,4,128]{3,2,0,1:T(4,128)}, u32[]{:S(2)}, u32[]{:S(2)}) async-start(f32[32,8,4,128]{3,2,0,1:T(4,128)} %copy.66), calls=%async_computation.3 | async-start | bytes 1048576 | tf_op jit(solution)/shard_map/all_to_all | solution.py:98
  126.1 5.9 %copy-start.7 = (f32[8,4,128]{2,1,0:T(4,128)S(1)}, f32[8,4,128]{2,1,0:T(4,128)}, u32[]{:S(2)}) copy-start(f32[8,4,128]{2,1,0:T(4,128)} %param.20) | copy-start | bytes 49156
  136.4 12.5 %all-to-all-start.2 = ((f32[32,8,4,128]{3,0,2,1:T(8,128)}), f32[32,8,4,128]{3,0,2,1:T(8,128)S(1)}, u32[]{:S(2)}, u32[]{:S(2)}) async-start(f32[32,8,4,128]{3,0,2,1:T(8,128)} %fusion.51), calls=%async_computation.2 | async-start | bytes 1048576 | tf_op jit(solution)/shard_map/all_to_all | solution.py:98
  243.1 11.1 %copy-start.1 = (f32[64,2048]{1,0:T(8,128)}, f32[64,2048]{1,0:T(8,128)S(1)}, u32[]{:S(2)}) copy-start(f32[64,2048]{1,0:T(8,128)S(1)} %fusion.147) | copy-start | bytes 1572868
  255.3 3.6 collective-permute-start.3
  258.9 0.7 copy-start.4
  280.9 16.2 %collective-permute-start.5 = (f32[32,6,4,128]{3,0,2,1:T(8,128)}, f32[32,6,4,128]{3,0,2,1:T(8,128)}, u32[]{:S(2)}, u32[]{:S(2)}) collective-permute-start(f32[32,6,4,128]{3,0,2,1:T(8,128)} %copy.95), channel_id=1, source_target_pairs={{0,1},{1,2},{2,3},{3,4},{4,5},{5,6},{6,7},{7,8},{8,9},{9,10},{10,1... | collective-permute-start | bytes 1179656 | tf_op jit(solution)/shard_map/ppermute | solution.py:38
  289.3 9.7 %collective-permute-start.4 = (f32[32,6,4,128]{3,0,2,1:T(8,128)}, f32[32,6,4,128]{3,0,2,1:T(8,128)}, u32[]{:S(2)}, u32[]{:S(2)}) collective-permute-start(f32[32,6,4,128]{3,0,2,1:T(8,128)} %get-tuple-element.38), channel_id=1, source_target_pairs={{0,1},{1,2},{2,3},{3,4},{4,5},{5,6},{6,7},{7,8},{8,9},{9,10},{10,1... | collective-permute-start | bytes 1179656 | tf_op jit(solution)/shard_map/ppermute | solution.py:27
  297.1 19.1 %copy-start.2 = (f32[64,2048]{1,0:T(8,128)S(1)}, f32[64,2048]{1,0:T(8,128)}, u32[]{:S(2)}) copy-start(f32[64,2048]{1,0:T(8,128)} %copy-done.1) | copy-start | bytes 1572868
  303.6 12.0 %all-to-all-start.5 = ((f32[32,8,4,128]{3,0,2,1:T(8,128)}), f32[32,8,4,128]{3,0,2,1:T(8,128)S(1)}, u32[]{:S(2)}, u32[]{:S(2)}) async-start(f32[32,8,4,128]{3,0,2,1:T(8,128)} %fusion.16), calls=%async_computation.5 | async-start | bytes 1048576 | tf_op jit(solution)/shard_map/all_to_all | solution.py:98
  412.4 11.0 %all-to-all-start.6 = ((f32[64,4,4,128]{3,2,1,0:T(4,128)}), f32[64,4,4,128]{3,2,1,0:T(4,128)S(1)}, u32[]{:S(2)}, u32[]{:S(2)}) async-start(f32[64,4,4,128]{3,2,1,0:T(4,128)} %reshape.195), calls=%async_computation.6 | async-start | bytes 1048576 | tf_op jit(solution)/shard_map/all_to_all | solution.py:101
where the time goes:
time: 426 us; the launch traced here: 424 us
  blocking collectives  209 us (49%)
  other arithmetic  66.8 us (16%)
  local copies, waits for them, and re-layouts  48.4 us (11%)
  starting transfers between devices  46.1 us (11%)
  waiting for transfers between devices  42.7 us (10%)
  matrix products  9.61 us (2%)
    psum x5, blocking collectives, summed(): return lax.psum(matrix, ('band', 'grid'))  198 us
    all_to_all x4, waiting for transfers between devices, to_cells(): lax.all_to_all(block, 'band', split_axis=1, concat_axis=0, tiled=True)  24 us
    another operation x9, other arithmetic, factor_of(): factor = jnp.linalg.cholesky(gram)  19.6 us
    ppermute x2, starting transfers between devices, from_behind(): return lax.ppermute(block, axis, route)  16.7 us
    another operation x6, other arithmetic, factor_of(): inverse = jax.scipy.linalg.solve_triangular(factor, identity, lower=True)  16.6 us
    scatter-add x2, other arithmetic, projector_terms(): jnp.zeros_like(extended).at[:, cell_list]  16 us
    all_to_all x4, starting transfers between devices, to_cells(): lax.all_to_all(block, 'band', split_axis=1, concat_axis=0, tiled=True)  15.7 us
    unnamed x28, local copies, waits for them, and re-layouts  14.7 us
  transfers between devices with their start and end apart: 12, of which 7 were waited for; matrix products, arithmetic and copies ran while one was open for 5% of the time, Pallas kernels for 0%

commit v1 on v0

v1 whole, which is shorter than its diff:
```python
import functools

import jax
import jax.numpy as jnp
from jax import lax
from jax.experimental import pallas as pl
from jax.experimental.pallas import tpu as pltpu
from jax.sharding import PartitionSpec as P

NB = 64
STEPS = 2
HALO = 6
MESH = pl.DeviceIdType.MESH

HIGHEST = lax.Precision.HIGHEST
STENCIL_WEIGHTS = (
    -5369.0 / 1800.0,
    12.0 / 7.0,
    -15.0 / 56.0,
    10.0 / 189.0,
    -1.0 / 112.0,
    2.0 / 1925.0,
    -1.0 / 16632.0,
)
HOP = tuple(-0.5 * w for w in STENCIL_WEIGHTS)
SHIFT = 3.0 * HOP[0]
BLOCKS = 5
PAIRS = [(i, j) for i in range(BLOCKS) for j in range(i, BLOCKS)]
F32 = jnp.float32
BF16 = jnp.bfloat16


def split(x):
    high = x.astype(BF16)
    return high, (x - high.astype(F32)).astype(BF16)


def dot_nt(a, b):
    return lax.dot_general(a, b, (((1,), (1,)), ((), ())), preferred_element_type=F32)


def dot_nn(a, b):
    return lax.dot_general(a, b, (((1,), (0,)), ((), ())), preferred_element_type=F32)


def krylov_kernel(
    nb, ng, planes, wy, slots, nproj, owners,
    x_ref, p_ref, pot_ref, cells_ref, proj_ref, scale_ref,
    s_ref, g_ref,
    ext, fin, dens_h, dens_l, prev_h, prev_l, prev_cells, prev_proj,
    csend, cprev, gpart, grecv, gown,
    halo_send, halo_recv, meta_send, meta_recv, c_send, c_recv,
    band_send, band_recv, rs_send, rs_recv, ag_send, ag_recv,
):
    ndev = nb * ng
    states = x_ref.shape[0] // (planes * wy)
    lines = planes * wy
    edge = HALO * wy
    part = lines // nb
    rows = slots * nproj
    wz = x_ref.shape[1]
    span = wy * wz
    band = lax.axis_index("band")
    grid = lax.axis_index("grid")
    me = band * ng + grid
    has_prev = grid > 0
    has_next = grid < ng - 1
    before = (band, jnp.maximum(grid - 1, 0))
    behind = (band, jnp.minimum(grid + 1, ng - 1))

    barrier = pltpu.get_barrier_semaphore()

    def greet(d, carry):
        t = lax.rem(me + d, ndev)
        pl.semaphore_signal(barrier, inc=1, device_id=(t // ng, lax.rem(t, ng)), device_id_type=MESH)
        return carry

    lax.fori_loop(1, ndev, greet, 0)

    def load(i, carry):
        ext[0, edge + i] = x_ref[pl.ds(i, states, stride=lines), :]
        ext[1, edge + i] = p_ref[pl.ds(i, states, stride=lines), :]
        return carry

    lax.fori_loop(0, lines, load, 0)

    @pl.when(jnp.logical_not(has_prev))
    def _():
        for b in range(3):
            ext[b, 0:edge] = jnp.zeros((edge, states, wz), F32)
            cprev[b] = jnp.zeros_like(cprev[b])
        prev_cells[...] = jnp.zeros_like(prev_cells)
        prev_proj[...] = jnp.zeros_like(prev_proj)

    @pl.when(jnp.logical_not(has_next))
    def _():
        for b in range(3):
            ext[b, edge + lines :] = jnp.zeros((edge, states, wz), F32)

    def dense(cells, proj, first, count, out_h, out_l):
        per = 8 // nproj
        line_iota = lax.broadcasted_iota(jnp.int32, (count, 8, per * wz), 0) + first
        lane_iota = lax.broadcasted_iota(jnp.int32, (wz, per * wz), 0)
        row_iota = lax.broadcasted_iota(jnp.int32, (8, wz), 0)
        for q in range(slots // per):
            values = proj[8 * q : 8 * q + 8, :]
            spread = jnp.concatenate(
                [jnp.where(row_iota // nproj == u, values, 0.0) for u in range(per)], axis=1
            )
            where = jnp.concatenate(
                [cells[per * q + u : per * q + u + 1, :] for u in range(per)], axis=1
            )
            hot = jnp.where(lane_iota == where % wz, 1.0, 0.0).astype(BF16)
            hit = line_iota == (where // wz)[None]
            for source, out in zip(split(spread), (out_h, out_l)):
                left = jnp.where(hit, source.astype(F32)[None], 0.0)
                left = left.reshape(count * 8, per * wz).astype(BF16)
                made = dot_nt(left, hot).reshape(count, 8, wz)
                out[0:count, 8 * q : 8 * q + 8, :] = made

    dense(cells_ref, proj_ref, 0, lines + edge, dens_h, dens_l)

    pl.semaphore_wait(barrier, ndev - 1)

    def up_copy(b):
        return pltpu.make_async_remote_copy(
            ext.at[b, pl.ds(lines, edge)], ext.at[b, pl.ds(0, edge)],
            halo_send.at[2 * b], halo_recv.at[2 * b], behind, MESH)

    def down_copy(b):
        return pltpu.make_async_remote_copy(
            ext.at[b, pl.ds(edge, edge)], ext.at[b, pl.ds(edge + lines, edge)],
            halo_send.at[2 * b + 1], halo_recv.at[2 * b + 1], before, MESH)

    def meta_copies():
        return (
            pltpu.make_async_remote_copy(
                cells_ref, prev_cells, meta_send.at[0], meta_recv.at[0], behind, MESH),
            pltpu.make_async_remote_copy(
                proj_ref, prev_proj, meta_send.at[1], meta_recv.at[1], behind, MESH),
        )

    def c_copy(b):
        return pltpu.make_async_remote_copy(
            csend.at[b], cprev.at[b], c_send.at[b], c_recv.at[b], behind, MESH)

    def start_halo(b):
        @pl.when(has_next)
        def _():
            up_copy(b).start()

        @pl.when(has_prev)
        def _():
            down_copy(b).start()

    def block_lines(b):
        return (ext.at[b], edge) if b < 3 else (fin.at[b - 3], 0)

    def band_copy(b, d):
        t = lax.rem(band + d, nb)
        ref, base = block_lines(b)
        return pltpu.make_async_remote_copy(
            ref.at[pl.ds(base + part * t, part)],
            s_ref.at[b, :, pl.ds(pl.multiple_of(band * states, states), states), :],
            band_send.at[b, d - 1], band_recv.at[b, d - 1], (t, grid), MESH)

    def start_band(b):
        for d in range(1, nb):
            band_copy(b, d).start()
        ref, base = block_lines(b)
        s_ref[b, :, pl.ds(pl.multiple_of(band * states, states), states), :] = ref[
            pl.ds(base + part * band, part)]

    @pl.when(has_next)
    def _():
        for copy in meta_copies():
            copy.start()

    start_halo(0)
    start_band(0)
    start_halo(1)
    start_band(1)

    @pl.when(has_prev)
    def _():
        for copy in meta_copies():
            copy.wait_recv()

    prev_h[edge:lines] = jnp.zeros((lines - edge, rows, wz), F32)
    prev_l[edge:lines] = jnp.zeros((lines - edge, rows, wz), F32)
    dense(prev_cells, prev_proj, lines, edge, prev_h, prev_l)

    lane = lax.broadcasted_iota(jnp.int32, (1, wz), 1)
    ups = [jnp.where(lane >= k, HOP[k], 0.0).astype(F32) for k in range(1, 7)]
    downs = [jnp.where(lane < wz - k, HOP[k], 0.0).astype(F32) for k in range(1, 7)]

    def wide(ref, first):
        return jnp.concatenate([ref[first + y] for y in range(wy)], axis=1)

    def apply(b, store):
        @pl.when(has_prev)
        def _():
            up_copy(b).wait_recv()

        @pl.when(has_next)
        def _():
            down_copy(b).wait_recv()

        def project(p, carry):
            value = jnp.concatenate([ext[b, edge + wy * p + y] for y in range(wy)], axis=1)
            high, low = split(value)
            d_h = wide(dens_h, wy * p).astype(BF16)
            d_l = wide(dens_l, wy * p).astype(BF16)
            both = dot_nt(high, d_h) + dot_nt(low, d_h)
            return carry + both + dot_nt(high, d_l)

        coefficient = lax.fori_loop(
            0, planes + HALO, project, jnp.zeros((states, rows), F32), unroll=2)
        scaled = coefficient * scale_ref[...]
        csend[b, :, 0:rows] = scaled

        @pl.when(has_next)
        def _():
            c_copy(b).start()

        own_h, own_l = split(scaled)

        def plane(p, carry):
            here = edge + wy * p
            center = [ext[b, here + y] for y in range(wy)]
            d_h = wide(dens_h, wy * p).astype(BF16)
            d_l = wide(dens_l, wy * p).astype(BF16)
            term = dot_nn(own_h, d_h) + dot_nn(own_l, d_h) + dot_nn(own_h, d_l)
            for y in range(wy):
                v = center[y]
                total = pot_ref[pl.ds(wy * p + y, 1), :] * v + term[:, y * wz : (y + 1) * wz]
                for k in range(1, 7):
                    total = total + HOP[k] * (
                        ext[b, here + wy * k + y] + ext[b, here - wy * k + y])
                for other in range(wy):
                    if 0 < abs(other - y) <= 6:
                        total = total + HOP[abs(other - y)] * center[other]
                for k in range(1, 7):
                    total = total + ups[k - 1] * pltpu.roll(v, k, 1)
                    total = total + downs[k - 1] * pltpu.roll(v, wz - k, 1)
                store(wy * p + y, total)
            return carry

        lax.fori_loop(0, planes, plane, 0)

        @pl.when(has_prev)
        def _():
            c_copy(b).wait_recv()

        got_h, got_l = split(cprev[b, :, 0:rows])

        def outer(p, carry):
            d_h = wide(prev_h, wy * p).astype(BF16)
            d_l = wide(prev_l, wy * p).astype(BF16)
            term = dot_nn(got_h, d_h) + dot_nn(got_l, d_h) + dot_nn(got_h, d_l)
            for y in range(wy):
                store(wy * p + y, term[:, y * wz : (y + 1) * wz], True)
            return carry

        lax.fori_loop(0, HALO, outer, 0)

    def store_to(ref, base):
        def store(i, value, add=False):
            if add:
                ref[base + i] = ref[base + i] + value
            else:
                ref[base + i] = value
        return store

    apply(0, store_to(ext.at[2], edge))
    start_halo(2)
    start_band(2)
    apply(1, store_to(fin.at[0], 0))
    start_band(3)
    apply(2, store_to(fin.at[1], 0))
    start_band(4)

    for b in range(BLOCKS):
        for d in range(1, nb):
            band_copy(b, d).wait_recv()

    many = 4 if part % 4 == 0 else 1

    def gram(i, carry):
        value = jnp.concatenate(
            [
                jnp.concatenate([s_ref[b, many * i + u] for b in range(BLOCKS)], axis=0)
                for u in range(many)
            ],
            axis=1,
        )
        high, low = split(value)
        return carry + dot_nt(high, high) + dot_nt(high, low) + dot_nt(low, high)

    total = lax.fori_loop(
        0, part // many, gram, jnp.zeros((BLOCKS * NB, BLOCKS * NB), F32))
    for n, (i, j) in enumerate(PAIRS):
        gpart[NB * (n // 2) : NB * (n // 2) + NB, NB * (n % 2) : NB * (n % 2) + NB] = total[
            NB * i : NB * i + NB, NB * j : NB * j + NB]
    gpart[NB * 7 :, NB:] = jnp.zeros((NB, NB), F32)

    share = gpart.shape[0] // owners

    def piece(index):
        return pl.ds(pl.multiple_of(index * share, share), share)

    def device(t):
        return (t // ng, lax.rem(t, ng))

    def rs_copy(d):
        t = lax.rem(me + d, ndev)
        return t, pltpu.make_async_remote_copy(
            gpart.at[piece(jnp.minimum(t, owners - 1))], grecv.at[d - 1],
            rs_send.at[d - 1], rs_recv.at[d - 1], device(t), MESH)

    def ag_copy(d, source):
        t = lax.rem(me + d, ndev)
        mine = piece(jnp.minimum(source, owners - 1))
        return pltpu.make_async_remote_copy(
            gown, g_ref.at[mine], ag_send.at[d - 1], ag_recv.at[d - 1], device(t), MESH)

    def guard(cond, body):
        if owners == ndev:
            body()
        else:
            pl.when(cond)(body)

    def rs_start(d, carry):
        t, copy = rs_copy(d)
        guard(t < owners, lambda: copy.start())
        return carry

    lax.fori_loop(1, ndev, rs_start, 0)

    def own_sum():
        def add(d, acc):
            _, copy = rs_copy(d)
            copy.wait_recv()
            return acc + grecv[d - 1]

        summed = lax.fori_loop(1, ndev, add, gpart[piece(jnp.minimum(me, owners - 1)), :])
        gown[...] = summed
        g_ref[piece(jnp.minimum(me, owners - 1)), :] = summed

        def ag_start(d, carry):
            ag_copy(d, me).start()
            return carry

        lax.fori_loop(1, ndev, ag_start, 0)

    guard(me < owners, own_sum)

    def ag_wait(d, carry):
        source = lax.rem(me + ndev - d, ndev)
        guard(source < owners, lambda: ag_copy(d, source).wait_recv())
        return carry

    lax.fori_loop(1, ndev, ag_wait, 0)

    def drain(d, carry):
        t, copy = rs_copy(d)
        guard(t < owners, lambda: copy.wait_send())
        guard(me < owners, lambda: ag_copy(d, me).wait_send())
        return carry

    lax.fori_loop(1, ndev, drain, 0)

    for b in range(BLOCKS):
        for d in range(1, nb):
            band_copy(b, d).wait_send()

    @pl.when(has_next)
    def _():
        for b in range(3):
            up_copy(b).wait_send()
            c_copy(b).wait_send()
        for copy in meta_copies():
            copy.wait_send()

    @pl.when(has_prev)
    def _():
        for b in range(3):
            down_copy(b).wait_send()


def final_kernel(nb, ng, m_ref, s_ref, q_ref, mine, got, sends, recvs):
    band = lax.axis_index("band")
    grid = lax.axis_index("grid")
    part = s_ref.shape[1]
    states = NB // nb
    lines = part * nb
    barrier = pltpu.get_barrier_semaphore()
    for d in range(1, nb):
        pl.semaphore_signal(
            barrier, inc=1, device_id=(lax.rem(band + d, nb), grid), device_id_type=MESH)
    high, low = split(m_ref[...])

    def combine(i, carry):
        value = jnp.concatenate([s_ref[b, i] for b in range(BLOCKS)], axis=0)
        v_h, v_l = split(value)
        made = dot_nn(high, v_h) + dot_nn(low, v_h) + dot_nn(high, v_l)
        for t in range(nb):
            mine[t, i] = made[t * states : (t + 1) * states]
        return carry

    lax.fori_loop(0, part, combine, 0, unroll=2)
    pl.semaphore_wait(barrier, nb - 1)

    def copy(d):
        t = lax.rem(band + d, nb)
        return pltpu.make_async_remote_copy(
            mine.at[t], got.at[band], sends.at[d - 1], recvs.at[d - 1], (t, grid), MESH)

    for d in range(1, nb):
        copy(d).start()

    def put(source, ref):
        def line(i, carry):
            q_ref[pl.ds(source * part + i, states, stride=lines), :] = ref[i]
            return carry

        lax.fori_loop(0, part, line, 0)

    put(band, mine.at[band])
    for d in range(1, nb):
        copy(d).wait_recv()
        source = lax.rem(band + nb - d, nb)
        put(source, got.at[source])
    for d in range(1, nb):
        copy(d).wait_send()


def factor_of(gram):
    factor = jnp.linalg.cholesky(gram)
    identity = jnp.eye(gram.shape[0], dtype=F32)
    inverse = jax.scipy.linalg.solve_triangular(factor, identity, lower=True)
    return (factor, inverse)


def mm(*factors):
    value = factors[0]
    for other in factors[1:]:
        value = jnp.dot(value, other, precision=HIGHEST)
    return value


def shards(
    start_block,
    previous_block,
    previous_coupling,
    potential,
    atom_cells,
    atom_proj,
    atom_strength,
    atom_count,
):
    states, planes, wy, wz = start_block.shape
    slots, nproj, points = atom_proj.shape
    nb, ng = lax.axis_size("band"), lax.axis_size("grid")
    ndev = nb * ng
    lines = planes * wy
    edge = HALO * wy
    part = lines // nb
    rows = slots * nproj
    cell_total = lines * ng * wz
    owners = min(ndev, 64)
    live = (jnp.arange(slots, dtype=jnp.int32) < atom_count[0]).astype(F32)
    scale = (atom_strength * live[:, None]).reshape(1, rows)
    dma = pltpu.SemaphoreType.DMA
    vmem = pl.BlockSpec(memory_space=pltpu.VMEM)
    grows = NB * 8
    basis, packed = pl.pallas_call(
        functools.partial(krylov_kernel, nb, ng, planes, wy, slots, nproj, owners),
        out_shape=(
            jax.ShapeDtypeStruct((BLOCKS, part, NB, wz), F32),
            jax.ShapeDtypeStruct((grows, 2 * NB), F32),
        ),
        in_specs=[vmem] * 6,
        out_specs=(vmem, vmem),
        scratch_shapes=[
            pltpu.VMEM((3, lines + 2 * edge, states, wz), F32),
            pltpu.VMEM((2, lines, states, wz), F32),
            pltpu.VMEM((lines + edge, rows, wz), F32),
            pltpu.VMEM((lines + edge, rows, wz), F32),
            pltpu.VMEM((lines, rows, wz), F32),
            pltpu.VMEM((lines, rows, wz), F32),
            pltpu.VMEM((slots, points), jnp.int32),
            pltpu.VMEM((rows, points), F32),
            pltpu.VMEM((3, states, 128), F32),
            pltpu.VMEM((3, states, 128), F32),
            pltpu.VMEM((grows, 2 * NB), F32),
            pltpu.VMEM((ndev - 1, grows // owners, 2 * NB), F32),
            pltpu.VMEM((grows // owners, 2 * NB), F32),
            dma((6,)), dma((6,)), dma((2,)), dma((2,)), dma((3,)), dma((3,)),
            dma((BLOCKS, nb - 1)), dma((BLOCKS, nb - 1)),
            dma((ndev - 1,)), dma((ndev - 1,)), dma((ndev - 1,)), dma((ndev - 1,)),
        ],
        compiler_params=pltpu.CompilerParams(
            collective_id=0, has_side_effects=True, vmem_limit_bytes=48 * 2**20),
    )(
        start_block.reshape(states * lines, wz),
        previous_block.reshape(states * lines, wz),
        potential.reshape(lines, wz),
        atom_cells,
        atom_proj.reshape(rows, points),
        scale,
    )
    packed = packed / cell_total
    g = {}
    for n, (i, j) in enumerate(PAIRS):
        block = packed[NB * (n // 2) : NB * (n // 2) + NB, NB * (n % 2) : NB * (n % 2) + NB]
        g[i, j] = block
        if i != j:
            g[j, i] = block.T
    whole = jnp.concatenate(
        [jnp.concatenate([g[i, j] for j in range(BLOCKS)], axis=1) for i in range(BLOCKS)], axis=0)
    zero = jnp.zeros((NB, NB), F32)
    factor, inverse = factor_of(g[0, 0])
    row = lambda *parts: jnp.concatenate(parts, axis=1)
    identity = jnp.eye(NB, dtype=F32)
    a_shifted = mm(inverse, g[0, 2], inverse.T)
    w0 = row(-mm(a_shifted.T, inverse), -previous_coupling, inverse, zero, zero)
    factor, inverse1 = factor_of(mm(w0, whole, w0.T))
    q0 = row(inverse, zero, zero, zero, zero)
    q1 = mm(inverse1, w0)
    hq1 = row(zero, zero, q1[:, :NB], q1[:, NB : 2 * NB], q1[:, 2 * NB : 3 * NB])
    a1_shifted = mm(q1, whole, hq1.T)
    coupling = factor.T
    w1 = hq1 - mm(a1_shifted.T, q1) - mm(coupling, q0)
    factor1, inverse2 = factor_of(mm(w1, whole, w1.T))
    q2 = mm(inverse2, w1)
    final = pl.pallas_call(
        functools.partial(final_kernel, nb, ng),
        out_shape=jax.ShapeDtypeStruct((states * lines, wz), F32),
        in_specs=[vmem] * 2,
        out_specs=vmem,
        scratch_shapes=[
            pltpu.VMEM((nb, part, states, wz), F32),
            pltpu.VMEM((nb, part, states, wz), F32),
            dma((nb - 1,)), dma((nb - 1,)),
        ],
        compiler_params=pltpu.CompilerParams(
            collective_id=1, has_side_effects=True, vmem_limit_bytes=32 * 2**20),
    )(q2, basis)
    offset = lax.axis_index("band") * states
    pick = lambda m: lax.dynamic_slice_in_dim(m, offset, states, 1)
    a_list = [pick(a_shifted + SHIFT * identity), pick(a1_shifted + SHIFT * identity)]
    b_list = [pick(factor.T), pick(factor1.T)]
    return (jnp.stack(a_list), jnp.stack(b_list), final.reshape(start_block.shape))


def solution(mesh):
    in_specs = (
        P("band", "grid", None, None),
        P("band", "grid", None, None),
        P(),
        P("grid", None, None),
        P("grid", None),
        P("grid", None, None),
        P("grid", None),
        P("grid"),
    )
    out_specs = (P(None, None, "band"), P(None, None, "band"), P("band", "grid", None, None))
    return jax.shard_map(shards, mesh=mesh, in_specs=in_specs, out_specs=out_specs, check_vma=False)
```

time: 426 us -> 144 us (0.34)
  blocking collectives: 209 us -> 0 us
  Pallas kernels: 0 us -> 75.8 us
  starting transfers between devices: 46.1 us -> 0 us
  waiting for transfers between devices: 42.7 us -> 0 us
  local copies, waits for them, and re-layouts: 48.4 us -> 19.1 us
  other arithmetic: 66.8 us -> 41.4 us
  matrix products: 9.61 us -> 4.9 us
    psum x5 -> x0, blocking collectives: 198 us -> none  [summed(): return lax.psum(matrix, ('band', 'grid'))]
    pallas_call x0 -> x2, Pallas kernels: none -> 75.8 us  [the longest x1 65.9 us: shards(): pl.pallas_call(functools.partial(krylov_kernel, nb, ng, planes, wy, slots...]
    all_to_all x6 -> x0, waiting for transfers between devices: 38.1 us -> none  [the longest x4 24 us: to_cells(): lax.all_to_all(block, 'band', split_axis=1, concat_axis=0, tiled=True)]
    ppermute x6 -> x0, starting transfers between devices: 23.3 us -> none  [the longest x2 16.7 us: from_behind(): return lax.ppermute(block, axis, route)]
    all_to_all x6 -> x0, starting transfers between devices: 22.8 us -> none  [the longest x4 15.7 us: to_cells(): lax.all_to_all(block, 'band', split_axis=1, concat_axis=0, tiled=True)]
    scatter-add x4 -> x0, other arithmetic: 19.9 us -> none  [the longest x2 16 us: projector_terms(): jnp.zeros_like(extended).at[:, cell_list]]
    slice x6 -> x4, local copies, waits for them, and re-layouts: 11.9 us -> 0.92 us  [the longest x3 0.91 us: shards(): packed[NB * (n // 2):NB * (n // 2) + NB, NB * (n % 2):NB * (n % 2) + NB]]
    all_to_all x1 -> x0, blocking collectives: 10.8 us -> none  [to_states(): lax.all_to_all(block, 'band', split_axis=0, concat_axis=1, tiled=True)]
  transfers between devices with their start and end apart: 12 -> 0, of which waited for: 7 -> 0; matrix products, arithmetic and copies ran while one was open for 5% -> 0% of each run, Pallas kernels for 0% -> 0%
where the time goes in v1:
time: 144 us; the launch traced here: 143 us
  Pallas kernels  75.8 us (53%)
  other arithmetic  41.4 us (29%)
  local copies, waits for them, and re-layouts  19.1 us (13%)
  matrix products  4.9 us (3%)
  between operations  1.57 us (1%)
    pallas_call x1, Pallas kernels, shards(): pl.pallas_call(functools.partial(krylov_kernel, nb, ng, planes, wy, slots...  65.9 us
    another operation x9, other arithmetic, factor_of(): factor = jnp.linalg.cholesky(gram)  19.6 us
    another operation x6, other arithmetic, factor_of(): inverse = jax.scipy.linalg.solve_triangular(factor, identity, lower=True)  16.6 us
    unnamed x23, local copies, waits for them, and re-layouts  14 us
    pallas_call x1, Pallas kernels, shards(): pl.pallas_call(functools.partial(final_kernel, nb, ng), out_shape=jax.Sha...  9.93 us
    dot_general x13, matrix products, mm(): value = jnp.dot(value, other, precision=HIGHEST)  4.15 us

profile of v1, /device:TPU:0, one launch (start us, length us, event | category | flops | bytes accessed | tf_op | source)
XLA Modules:
  0.0 142.7 jit_solution(12015704441654431002)
XLA Ops:
  1.3 0.7 broadcast_multiply_fusion.1
  2.1 1.0 copy-done
  3.2 1.0 copy-done.1
  4.2 0.7 copy-done.2
  4.9 0.7 copy-done.3
  5.7 0.7 copy-done.4
  6.4 65.9 %shard_map.103 = (f32[5,16,64,128]{3,2,1,0:T(8,128)S(1)}, f32[512,128]{1,0:T(8,128)S(1)}) custom-call(f32[1024,128]{1,0:T(8,128)S(1)} %bitcast.81, f32[1024,128]{1,0:T(8,128)S(1)} %bitcast.82, f32[32,128]{1,0:T(8,128)S(1)} %bitcast.83, s32[8,128]{1,0:T(8,128)S(1)} %copy-done.4, f32[32,128]{1,0:T(8,128)S(1)} %bitcast.84, f32[1,32]{1,0:T(1,128)S(1)} %reshape.41.scale_ref), custom_call_target="tpu_custom_call" | custom-call | tf_op jit(solution)/shard_map/pallas_call | solution.py:477
  72.4 0.7 fusion.29
  73.2 5.8 %cholesky.59 = f32[64,64]{1,0:T(8,128)S(1)} custom-call(f32[64,64]{1,0:T(8,128)S(1)} %fusion.15), custom_call_target="Cholesky" | custom-call | tf_op jit(solution)/shard_map/jit(cholesky)/cholesky | solution.py:439
  79.1 0.7 compare_reduce_fusion.2
  79.8 0.6 fusion.9
  80.5 4.9 %custom-call.7 = f32[1,64,64]{1,2,0:T(8,128)S(1)} custom-call(f32[1,64,64]{2,1,0:T(8,128)S(1)} %fusion.9), custom_call_target="InvertDiagBlocksLowerTriangular" | custom-call | tf_op jit(solution)/shard_map/jit(_solve_triangular)/triangular_solve | solution.py:441
  86.2 0.7 copy.41
  86.9 0.7 copy.43
  87.6 0.7 copy.44
  88.3 0.7 copy.45
  89.0 0.7 copy.46
  89.8 0.9 pad_maximum_fusion.2
  90.6 1.4 %copy.42 = f32[64,64]{1,0:T(8,128)} copy(f32[64,64]{0,1:T(8,128)} %get-tuple-element.21) | data formatting | bytes 32768
  92.1 1.5 %pad_maximum_fusion = (f32[64,320]{0,1:T(8,128)}, f32[64,320]{0,1:T(8,128)}) fusion(f32[64,64]{0,1:T(8,128)} %get-tuple-element.26, f32[64,128]{0,1:T(8,128)S(1)} %get-tuple-element.31, f32[64,128]{0,1:T(8,128)S(1)} %get-tuple-element.32, f32[64,64]{0,1:T(8,128)S(1)} %get-tuple-element.24, f32[64,128]{0,1:T(8,128)S(1)} %get-tuple-element.30, ...), kind=kLoop, calls=%fused_computation.3 | loop fusion | flops 102400 | bytes 327680 | tf_op jit(solution)/shard_map/concatenate | solution.py:521
  93.6 0.8 copy.37
  94.4 0.6 constant_dynamic-update-slice_fusion.1
  95.1 0.8 copy.38
  95.9 0.6 constant_dynamic-update-slice_fusion
  96.5 0.8 copy.47
  97.3 0.6 bitcast_dynamic-update-slice_fusion.1
  98.0 0.8 copy.48
  98.8 0.6 bitcast_dynamic-update-slice_fusion
  99.4 0.7 slice_dynamic-update-slice_fusion
  100.1 1.3 concatenate.39
  101.4 0.8 neg.7
  102.2 0.6 fusion.19
  102.8 0.3 fusion.18
  103.2 5.8 %cholesky.70 = f32[64,64]{1,0:T(8,128)S(1)} custom-call(f32[64,64]{1,0:T(8,128)S(1)} %fusion.13), custom_call_target="Cholesky" | custom-call | tf_op jit(solution)/shard_map/jit(cholesky)/cholesky | solution.py:439
  109.1 0.6 compare_reduce_fusion.1
  109.7 0.7 select_bitcast_fusion.1
  110.4 4.9 %custom-call.8 = f32[1,64,64]{1,2,0:T(8,128)S(1)} custom-call(f32[1,64,64]{2,1,0:T(8,128)S(1)} %get-tuple-element.11), custom_call_target="InvertDiagBlocksLowerTriangular" | custom-call | tf_op jit(solution)/shard_map/jit(_solve_triangular)/triangular_solve | solution.py:441
  115.6 0.3 fusion.17
  115.9 0.6 fusion.32
  117.2 0.6 fusion.33
  118.2 5.8 %cholesky.81 = f32[64,64]{1,0:T(8,128)S(1)} custom-call(f32[64,64]{1,0:T(8,128)S(1)} %fusion.11), custom_call_target="Cholesky" | custom-call | tf_op jit(solution)/shard_map/jit(cholesky)/cholesky | solution.py:439
  124.0 0.6 compare_reduce_fusion
  124.7 0.7 select_bitcast_fusion
  125.3 4.9 %custom-call.9 = f32[1,64,64]{1,2,0:T(8,128)S(1)} custom-call(f32[1,64,64]{2,1,0:T(8,128)S(1)} %get-tuple-element.9), custom_call_target="InvertDiagBlocksLowerTriangular" | custom-call | tf_op jit(solution)/shard_map/jit(_solve_triangular)/triangular_solve | solution.py:441
  130.7 9.9 %shard_map.104 = f32[1024,128]{1,0:T(8,128)S(1)} custom-call(f32[64,320]{1,0:T(8,128)S(1)} %fusion.35.m_ref, f32[5,16,64,128]{3,2,1,0:T(8,128)S(1)} %get-tuple-element.8.s_ref), custom_call_target="tpu_custom_call" | custom-call | tf_op jit(solution)/shard_map/pallas_call | solution.py:537
  140.7 0.6 pad_maximum_fusion.5
  141.3 0.6 pad_maximum_fusion.4
  141.9 0.8 copy.55
  (38 shorter events, 3.4 us)
Async XLA Ops:
  2.1 1.0 copy-start
  3.2 1.0 copy-start.1
  4.2 0.7 copy-start.2
  4.9 0.7 copy-start.3
  5.7 0.7 copy-start.4

commit v2 on v1

--- a/solution.py
+++ b/solution.py
@@ -45,8 +45,10 @@
 
 def krylov_kernel(
     nb, ng, planes, wy, slots, nproj, owners,
-    x_ref, p_ref, pot_ref, cells_ref, proj_ref, scale_ref,
-    s_ref, g_ref,
+    x_hbm, p_hbm, pot_hbm, cells_hbm, proj_hbm, scale_hbm, prior_hbm,
+    small_ref, q_ref,
+    x_ref, p_ref, pot_ref, cells_ref, proj_ref, scale_ref, prior_ref, in_sems,
+    s_ref, g_ref, whole, co, mat, mine, got, out_send, out_recv,
     ext, fin, dens_h, dens_l, prev_h, prev_l, prev_cells, prev_proj,
     csend, cprev, gpart, grecv, gown,
     halo_send, halo_recv, meta_send, meta_recv, c_send, c_recv,
@@ -75,7 +77,17 @@
         pl.semaphore_signal(barrier, inc=1, device_id=(t // ng, lax.rem(t, ng)), device_id_type=MESH)
         return carry
 
+    loads = [
+        pltpu.make_async_copy(source, target, in_sems.at[n])
+        for n, (source, target) in enumerate((
+            (cells_hbm, cells_ref), (proj_hbm, proj_ref), (x_hbm, x_ref), (p_hbm, p_ref),
+            (pot_hbm, pot_ref), (scale_hbm, scale_ref), (prior_hbm, prior_ref)))
+    ]
+    for copy in loads:
+        copy.start()
     lax.fori_loop(1, ndev, greet, 0)
+    for copy in loads:
+        copy.wait()
 
     def load(i, carry):
         ext[0, edge + i] = x_ref[pl.ds(i, states, stride=lines), :]
@@ -102,21 +114,25 @@
         line_iota = lax.broadcasted_iota(jnp.int32, (count, 8, per * wz), 0) + first
         lane_iota = lax.broadcasted_iota(jnp.int32, (wz, per * wz), 0)
         row_iota = lax.broadcasted_iota(jnp.int32, (8, wz), 0)
-        for q in range(slots // per):
-            values = proj[8 * q : 8 * q + 8, :]
-            spread = jnp.concatenate(
-                [jnp.where(row_iota // nproj == u, values, 0.0) for u in range(per)], axis=1
-            )
-            where = jnp.concatenate(
-                [cells[per * q + u : per * q + u + 1, :] for u in range(per)], axis=1
-            )
-            hot = jnp.where(lane_iota == where % wz, 1.0, 0.0).astype(BF16)
-            hit = line_iota == (where // wz)[None]
-            for source, out in zip(split(spread), (out_h, out_l)):
-                left = jnp.where(hit, source.astype(F32)[None], 0.0)
-                left = left.reshape(count * 8, per * wz).astype(BF16)
-                made = dot_nt(left, hot).reshape(count, 8, wz)
-                out[0:count, 8 * q : 8 * q + 8, :] = made
+        for pair in range(slots // per // 2):
+            made = ([], [])
+            for q in (2 * pair, 2 * pair + 1):
+                values = proj[8 * q : 8 * q + 8, :]
+                spread = jnp.concatenate(
+                    [jnp.where(row_iota // nproj == u, values, 0.0) for u in range(per)], axis=1
+                )
+                where = jnp.concatenate(
+                    [cells[per * q + u : per * q + u + 1, :] for u in range(per)], axis=1
+                )
+                hot = jnp.where(lane_iota == where % wz, 1.0, 0.0).astype(BF16)
+                hit = line_iota == (where // wz)[None]
+                for source, out in zip(split(spread), made):
+                    left = jnp.where(hit, source.astype(F32)[None], 0.0)
+                    left = left.reshape(count * 8, per * wz).astype(BF16)
+                    out.append(dot_nt(left, hot).reshape(count, 8, wz))
+            for parts, out in zip(made, (out_h, out_l)):
+                out[0:count, 16 * pair : 16 * pair + 16, :] = jnp.concatenate(
+                    parts, axis=1).astype(BF16)
 
     dense(cells_ref, proj_ref, 0, lines + edge, dens_h, dens_l)
 
@@ -186,8 +202,6 @@
         for copy in meta_copies():
             copy.wait_recv()
 
-    prev_h[edge:lines] = jnp.zeros((lines - edge, rows, wz), F32)
-    prev_l[edge:lines] = jnp.zeros((lines - edge, rows, wz), F32)
     dense(prev_cells, prev_proj, lines, edge, prev_h, prev_l)
 
     lane = lax.broadcasted_iota(jnp.int32, (1, wz), 1)
@@ -209,8 +223,8 @@
         def project(p, carry):
             value = jnp.concatenate([ext[b, edge + wy * p + y] for y in range(wy)], axis=1)
             high, low = split(value)
-            d_h = wide(dens_h, wy * p).astype(BF16)
-            d_l = wide(dens_l, wy * p).astype(BF16)
+            d_h = wide(dens_h, wy * p)
+            d_l = wide(dens_l, wy * p)
             both = dot_nt(high, d_h) + dot_nt(low, d_h)
             return carry + both + dot_nt(high, d_l)
 
@@ -228,8 +242,8 @@
         def plane(p, carry):
             here = edge + wy * p
             center = [ext[b, here + y] for y in range(wy)]
-            d_h = wide(dens_h, wy * p).astype(BF16)
-            d_l = wide(dens_l, wy * p).astype(BF16)
+            d_h = wide(dens_h, wy * p)
+            d_l = wide(dens_l, wy * p)
             term = dot_nn(own_h, d_h) + dot_nn(own_l, d_h) + dot_nn(own_h, d_l)
             for y in range(wy):
                 v = center[y]
@@ -255,8 +269,8 @@
         got_h, got_l = split(cprev[b, :, 0:rows])
 
         def outer(p, carry):
-            d_h = wide(prev_h, wy * p).astype(BF16)
-            d_l = wide(prev_l, wy * p).astype(BF16)
+            d_h = wide(prev_h, wy * p)
+            d_l = wide(prev_l, wy * p)
             term = dot_nn(got_h, d_h) + dot_nn(got_l, d_h) + dot_nn(got_h, d_l)
             for y in range(wy):
                 store(wy * p + y, term[:, y * wz : (y + 1) * wz], True)
@@ -362,6 +376,96 @@
 
     lax.fori_loop(1, ndev, ag_wait, 0)
 
+    inverse_total = 1.0 / (lines * ng * wz)
+    for n, (i, j) in enumerate(PAIRS):
+        block = g_ref[NB * (n // 2) : NB * (n // 2) + NB, NB * (n % 2) : NB * (n % 2) + NB]
+        block = block * inverse_total
+        whole[NB * i : NB * i + NB, NB * j : NB * j + NB] = block
+        if i != j:
+            whole[NB * j : NB * j + NB, NB * i : NB * i + NB] = block.T
+
+    def full_nn(a, b):
+        return lax.dot_general(
+            a, b, (((1,), (0,)), ((), ())), precision=HIGHEST, preferred_element_type=F32)
+
+    def full_nt(a, b):
+        return lax.dot_general(
+            a, b, (((1,), (1,)), ((), ())), precision=HIGHEST, preferred_element_type=F32)
+
+    row = lax.broadcasted_iota(jnp.int32, (NB, NB), 0)
+    col = lax.broadcasted_iota(jnp.int32, (NB, NB), 1)
+    identity = jnp.where(row == col, 1.0, 0.0).astype(F32)
+
+    def factor(gram_matrix):
+        mat[:, 0:NB] = gram_matrix
+        mat[:, NB:] = identity
+        factor_in_place(mat)
+        return jnp.where(col >= row, mat[:, 0:NB], 0.0), mat[:, NB:]
+
+    _, inverse0 = factor(whole[0:NB, 0:NB])
+    half = full_nn(inverse0, whole[0:NB, 2 * NB : 3 * NB])
+    a0 = full_nt(half, inverse0)
+    co[:, 0:NB] = -full_nn(full_nt(inverse0, half), inverse0)
+    co[:, NB : 2 * NB] = -prior_ref[...]
+    co[:, 2 * NB : 3 * NB] = inverse0
+    w0 = co[:, 0 : 3 * NB]
+    upper1, inverse1 = factor(full_nt(full_nn(w0, whole[0 : 3 * NB, 0 : 3 * NB]), w0))
+    q1 = full_nn(inverse1, w0)
+    half = full_nn(q1, whole[0 : 3 * NB, 2 * NB : 5 * NB])
+    a1 = full_nt(half, q1)
+    past = full_nn(full_nt(q1, half), q1)
+    co[:, 2 * NB : 5 * NB] = q1
+    co[:, 0:NB] = -past[:, 0:NB] - full_nn(upper1, inverse0)
+    co[:, NB : 2 * NB] = -past[:, NB : 2 * NB]
+    co[:, 2 * NB : 3 * NB] = co[:, 2 * NB : 3 * NB] - past[:, 2 * NB : 3 * NB]
+    w1 = co[...]
+    upper2, inverse2 = factor(full_nt(full_nn(w1, whole[...]), w1))
+    q2 = full_nn(inverse2, w1)
+
+    c_high, c_low = split(q2)
+    many = 2 if part % 2 == 0 else 1
+
+    def combine(i, carry):
+        value = jnp.concatenate(
+            [
+                jnp.concatenate([s_ref[b, many * i + u] for b in range(BLOCKS)], axis=0)
+                for u in range(many)
+            ],
+            axis=1,
+        )
+        v_h, v_l = split(value)
+        made = dot_nn(c_high, v_h) + dot_nn(c_low, v_h) + dot_nn(c_high, v_l)
+        for t in range(nb):
+            for u in range(many):
+                mine[t, many * i + u] = made[
+                    t * states : (t + 1) * states, u * wz : (u + 1) * wz]
+        return carry
+
+    lax.fori_loop(0, part // many, combine, 0, unroll=2 if part // many > 1 else 1)
+
+    def out_copy(d):
+        t = lax.rem(band + d, nb)
+        return pltpu.make_async_remote_copy(
+            mine.at[t], got.at[band], out_send.at[d - 1], out_recv.at[d - 1], (t, grid), MESH)
+
+    for d in range(1, nb):
+        out_copy(d).start()
+
+    def put(source, ref):
+        def line(i, carry):
+            q_ref[pl.ds(source * part + i, states, stride=lines), :] = ref[i]
+            return carry
+
+        lax.fori_loop(0, part, line, 0)
+
+    put(band, mine.at[band])
+    pick = jnp.where(
+        lax.broadcasted_iota(jnp.int32, (NB, states), 0)
+        == lax.broadcasted_iota(jnp.int32, (NB, states), 1) + band * states, 1.0, 0.0).astype(F32)
+    outs = (a0 + SHIFT * identity, a1 + SHIFT * identity, upper1, upper2)
+    for n, value in enumerate(outs):
+        small_ref[n] = full_nn(value, pick)
+
     def drain(d, carry):
         t, copy = rs_copy(d)
         guard(t < owners, lambda: copy.wait_send())
@@ -387,66 +491,41 @@
         for b in range(3):
             down_copy(b).wait_send()
 
-
-def final_kernel(nb, ng, m_ref, s_ref, q_ref, mine, got, sends, recvs):
-    band = lax.axis_index("band")
-    grid = lax.axis_index("grid")
-    part = s_ref.shape[1]
-    states = NB // nb
-    lines = part * nb
-    barrier = pltpu.get_barrier_semaphore()
     for d in range(1, nb):
-        pl.semaphore_signal(
-            barrier, inc=1, device_id=(lax.rem(band + d, nb), grid), device_id_type=MESH)
-    high, low = split(m_ref[...])
-
-    def combine(i, carry):
-        value = jnp.concatenate([s_ref[b, i] for b in range(BLOCKS)], axis=0)
-        v_h, v_l = split(value)
-        made = dot_nn(high, v_h) + dot_nn(low, v_h) + dot_nn(high, v_l)
-        for t in range(nb):
-            mine[t, i] = made[t * states : (t + 1) * states]
-        return carry
-
-    lax.fori_loop(0, part, combine, 0, unroll=2)
-    pl.semaphore_wait(barrier, nb - 1)
-
-    def copy(d):
-        t = lax.rem(band + d, nb)
-        return pltpu.make_async_remote_copy(
-            mine.at[t], got.at[band], sends.at[d - 1], recvs.at[d - 1], (t, grid), MESH)
-
-    for d in range(1, nb):
-        copy(d).start()
-
-    def put(source, ref):
-        def line(i, carry):
-            q_ref[pl.ds(source * part + i, states, stride=lines), :] = ref[i]
-            return carry
-
-        lax.fori_loop(0, part, line, 0)
-
-    put(band, mine.at[band])
-    for d in range(1, nb):
-        copy(d).wait_recv()
+        out_copy(d).wait_recv()
         source = lax.rem(band + nb - d, nb)
         put(source, got.at[source])
     for d in range(1, nb):
-        copy(d).wait_send()
-
-
-def factor_of(gram):
-    factor = jnp.linalg.cholesky(gram)
-    identity = jnp.eye(gram.shape[0], dtype=F32)
-    inverse = jax.scipy.linalg.solve_triangular(factor, identity, lower=True)
-    return (factor, inverse)
-
-
-def mm(*factors):
-    value = factors[0]
-    for other in factors[1:]:
-        value = jnp.dot(value, other, precision=HIGHEST)
-    return value
+        out_copy(d).wait_send()
+
+
+def factor_in_place(mat):
+    tall, width = mat.shape
+    tiles = [mat[8 * i : 8 * i + 8, :] for i in range(tall // 8)]
+    sublane = lax.broadcasted_iota(jnp.int32, (8, width), 0)
+    for j in range(tall // 8):
+        columns = [
+            {
+                i: jnp.broadcast_to(tiles[i][:, 8 * j + c : 8 * j + c + 1], (8, width))
+                for i in range(j, tall // 8)
+            }
+            for c in range(8)
+        ]
+        roots = jnp.ones((8, width), F32)
+        for c in range(8):
+            pivot = jnp.broadcast_to(columns[c][j][c : c + 1, :], (8, width))
+            line = jnp.broadcast_to(tiles[j][c : c + 1, :], (8, width))
+            roots = jnp.where(sublane == c, pivot, roots)
+            inverse = 1.0 / pivot
+            tops = {k: jnp.broadcast_to(columns[k][j][c : c + 1, :], (8, width)) for k in range(c + 1, 8)}
+            for i in range(j, tall // 8):
+                ratio = columns[c][i] * inverse
+                if i == j:
+                    ratio = jnp.where(sublane > c, ratio, 0.0)
+                tiles[i] = tiles[i] - ratio * line
+                for k in range(c + 1, 8):
+                    columns[k][i] = columns[k][i] - ratio * tops[k]
+        mat[8 * j : 8 * j + 8, :] = tiles[j] / jnp.sqrt(roots)
 
 
 def shards(
@@ -467,41 +546,57 @@
     edge = HALO * wy
     part = lines // nb
     rows = slots * nproj
-    cell_total = lines * ng * wz
     owners = min(ndev, 64)
     live = (jnp.arange(slots, dtype=jnp.int32) < atom_count[0]).astype(F32)
     scale = (atom_strength * live[:, None]).reshape(1, rows)
     dma = pltpu.SemaphoreType.DMA
     vmem = pl.BlockSpec(memory_space=pltpu.VMEM)
     grows = NB * 8
-    basis, packed = pl.pallas_call(
+    share = grows // owners
+    small, final = pl.pallas_call(
         functools.partial(krylov_kernel, nb, ng, planes, wy, slots, nproj, owners),
         out_shape=(
-            jax.ShapeDtypeStruct((BLOCKS, part, NB, wz), F32),
-            jax.ShapeDtypeStruct((grows, 2 * NB), F32),
+            jax.ShapeDtypeStruct((2 * STEPS, NB, states), F32),
+            jax.ShapeDtypeStruct((states * lines, wz), F32),
         ),
-        in_specs=[vmem] * 6,
+        in_specs=[pl.BlockSpec(memory_space=pl.ANY)] * 7,
         out_specs=(vmem, vmem),
         scratch_shapes=[
+            pltpu.VMEM((states * lines, wz), F32),
+            pltpu.VMEM((states * lines, wz), F32),
+            pltpu.VMEM((lines, wz), F32),
+            pltpu.VMEM((slots, points), jnp.int32),
+            pltpu.VMEM((rows, points), F32),
+            pltpu.VMEM((1, rows), F32),
+            pltpu.VMEM((NB, NB), F32),
+            dma((7,)),
+            pltpu.VMEM((BLOCKS, part, NB, wz), F32),
+            pltpu.VMEM((grows, 2 * NB), F32),
+            pltpu.VMEM((BLOCKS * NB, BLOCKS * NB), F32),
+            pltpu.VMEM((NB, BLOCKS * NB), F32),
+            pltpu.VMEM((NB, 2 * NB), F32),
+            pltpu.VMEM((nb, part, states, wz), F32),
+            pltpu.VMEM((nb, part, states, wz), F32),
+            dma((nb - 1,)), dma((nb - 1,)),
             pltpu.VMEM((3, lines + 2 * edge, states, wz), F32),
             pltpu.VMEM((2, lines, states, wz), F32),
-            pltpu.VMEM((lines + edge, rows, wz), F32),
-            pltpu.VMEM((lines + edge, rows, wz), F32),
-            pltpu.VMEM((lines, rows, wz), F32),
-            pltpu.VMEM((lines, rows, wz), F32),
+            pltpu.VMEM((lines + edge, rows, wz), BF16),
+            pltpu.VMEM((lines + edge, rows, wz), BF16),
+            pltpu.VMEM((edge, rows, wz), BF16),
+            pltpu.VMEM((edge, rows, wz), BF16),
             pltpu.VMEM((slots, points), jnp.int32),
             pltpu.VMEM((rows, points), F32),
             pltpu.VMEM((3, states, 128), F32),
             pltpu.VMEM((3, states, 128), F32),
             pltpu.VMEM((grows, 2 * NB), F32),
-            pltpu.VMEM((ndev - 1, grows // owners, 2 * NB), F32),
-            pltpu.VMEM((grows // owners, 2 * NB), F32),
+            pltpu.VMEM((ndev - 1, share, 2 * NB), F32),
+            pltpu.VMEM((share, 2 * NB), F32),
             dma((6,)), dma((6,)), dma((2,)), dma((2,)), dma((3,)), dma((3,)),
             dma((BLOCKS, nb - 1)), dma((BLOCKS, nb - 1)),
             dma((ndev - 1,)), dma((ndev - 1,)), dma((ndev - 1,)), dma((ndev - 1,)),
         ],
         compiler_params=pltpu.CompilerParams(
-            collective_id=0, has_side_effects=True, vmem_limit_bytes=48 * 2**20),
+            collective_id=0, has_side_effects=True, vmem_limit_bytes=60 * 2**20),
     )(
         start_block.reshape(states * lines, wz),
         previous_block.reshape(states * lines, wz),
@@ -509,49 +604,9 @@
         atom_cells,
         atom_proj.reshape(rows, points),
         scale,
+        previous_coupling,
     )
-    packed = packed / cell_total
-    g = {}
-    for n, (i, j) in enumerate(PAIRS):
-        block = packed[NB * (n // 2) : NB * (n // 2) + NB, NB * (n % 2) : NB * (n % 2) + NB]
-        g[i, j] = block
-        if i != j:
-            g[j, i] = block.T
-    whole = jnp.concatenate(
-        [jnp.concatenate([g[i, j] for j in range(BLOCKS)], axis=1) for i in range(BLOCKS)], axis=0)
-    zero = jnp.zeros((NB, NB), F32)
-    factor, inverse = factor_of(g[0, 0])
-    row = lambda *parts: jnp.concatenate(parts, axis=1)
-    identity = jnp.eye(NB, dtype=F32)
-    a_shifted = mm(inverse, g[0, 2], inverse.T)
-    w0 = row(-mm(a_shifted.T, inverse), -previous_coupling, inverse, zero, zero)
-    factor, inverse1 = factor_of(mm(w0, whole, w0.T))
-    q0 = row(inverse, zero, zero, zero, zero)
-    q1 = mm(inverse1, w0)
-    hq1 = row(zero, zero, q1[:, :NB], q1[:, NB : 2 * NB], q1[:, 2 * NB : 3 * NB])
-    a1_shifted = mm(q1, whole, hq1.T)
-    coupling = factor.T
-    w1 = hq1 - mm(a1_shifted.T, q1) - mm(coupling, q0)
-    factor1, inverse2 = factor_of(mm(w1, whole, w1.T))
-    q2 = mm(inverse2, w1)
-    final = pl.pallas_call(
-        functools.partial(final_kernel, nb, ng),
-        out_shape=jax.ShapeDtypeStruct((states * lines, wz), F32),
-        in_specs=[vmem] * 2,
-        out_specs=vmem,
-        scratch_shapes=[
-            pltpu.VMEM((nb, part, states, wz), F32),
-            pltpu.VMEM((nb, part, states, wz), F32),
-            dma((nb - 1,)), dma((nb - 1,)),
-        ],
-        compiler_params=pltpu.CompilerParams(
-            collective_id=1, has_side_effects=True, vmem_limit_bytes=32 * 2**20),
-    )(q2, basis)
-    offset = lax.axis_index("band") * states
-    pick = lambda m: lax.dynamic_slice_in_dim(m, offset, states, 1)
-    a_list = [pick(a_shifted + SHIFT * identity), pick(a1_shifted + SHIFT * identity)]
-    b_list = [pick(factor.T), pick(factor1.T)]
-    return (jnp.stack(a_list), jnp.stack(b_list), final.reshape(start_block.shape))
+    return (small[:STEPS], small[STEPS:], final.reshape(start_block.shape))
 
 
 def solution(mesh):

time: 144 us -> 91.4 us (0.63)
  other arithmetic: 41.4 us -> 0.01 us
  local copies, waits for them, and re-layouts: 19.1 us -> 5.47 us
  Pallas kernels: 75.8 us -> 84.3 us
  matrix products: 4.9 us -> 0 us
    another operation x18 -> x0, other arithmetic: 37.5 us -> none  [the longest x9 19.6 us: factor_of(): factor = jnp.linalg.cholesky(gram)]
    pallas_call x1, Pallas kernels: 65.9 us -> 84.3 us  [shards(): pl.pallas_call(functools.partial(krylov_kernel, nb, ng, planes, wy, slots...]
    unnamed x23 -> x5, local copies, waits for them, and re-layouts: 14 us -> 3.91 us
    pallas_call x1 -> x0, Pallas kernels: 9.93 us -> none  [shards(): pl.pallas_call(functools.partial(final_kernel, nb, ng), out_shape=jax.Sha...]
    dot_general x13 -> x0, matrix products: 4.15 us -> none  [mm(): value = jnp.dot(value, other, precision=HIGHEST)]
    concatenate x2 -> x0, other arithmetic: 2.39 us -> none  [shards(): jnp.concatenate([g[i, j] for j in range(BLOCKS)], axis=1)]
    concatenate x3 -> x0, local copies, waits for them, and re-layouts: 2.03 us -> none  [the longest x1 1.27 us: shards(): jnp.concatenate([jnp.concatenate([g[i, j] for j in range(BLOCKS)], axis=1...]
    transpose x2 -> x0, local copies, waits for them, and re-layouts: 1.66 us -> none  [shards(): g[j, i] = block.T]
where the time goes in v2:
time: 91.4 us; the launch traced here: 91.1 us
  Pallas kernels  84.3 us (92%)
  local copies, waits for them, and re-layouts  5.47 us (6%)
  between operations  1.31 us (1%)
    pallas_call x1, Pallas kernels, shards(): pl.pallas_call(functools.partial(krylov_kernel, nb, ng, planes, wy, slots...  84.3 us
    unnamed x5, local copies, waits for them, and re-layouts  3.91 us

profile of v2, /device:TPU:0, one launch (start us, length us, event | category | flops | bytes accessed | tf_op | source)
XLA Modules:
  0.0 91.1 jit_solution(15601256607302086420)
XLA Ops:
  1.3 0.0 copy-start
  1.3 0.7 copy-done
  2.0 0.1 copy.14
  2.0 0.6 reshape.33.scale_hbm
  2.6 84.3 %shard_map.103 = (f32[4,64,32]{2,1,0:T(8,128)}, f32[1024,128]{1,0:T(8,128)}) custom-call(f32[1024,128]{1,0:T(8,128)} %bitcast.7, f32[1024,128]{1,0:T(8,128)} %bitcast.8, f32[32,128]{1,0:T(8,128)} %bitcast.10, s32[8,128]{1,0:T(8,128)} %cells_hbm.1, f32[32,128]{1,0:T(8,128)} %bitcast.11, f32[1,32]{1,0:T(1,128)} %reshape.33.scale_hbm, f32[64,64]{1,0:T(8,128)} %prior_hbm.1), custom_call_target="tpu_custom_call" | custom-call | tf_op jit(solution)/shard_map/pallas_call | solution.py:556
  87.0 0.9 fusion
  87.9 0.7 copy.15
  88.6 0.7 copy.16
  89.3 1.9 %copy.19 = f32[32,8,4,128]{3,2,1,0:T(4,128)} copy(f32[32,8,4,128]{3,2,1,0:T(4,128)} %bitcast.9) | data formatting | bytes 1048576
  (2 shorter events, 0.0 us)
Async XLA Ops:
  1.3 0.7 copy-start

commit v3 on v2

--- a/solution.py
+++ b/solution.py
@@ -25,7 +25,11 @@
 HOP = tuple(-0.5 * w for w in STENCIL_WEIGHTS)
 SHIFT = 3.0 * HOP[0]
 BLOCKS = 5
-PAIRS = [(i, j) for i in range(BLOCKS) for j in range(i, BLOCKS)]
+FIRST = ((0, 0), (0, 1), (0, 2), (0, 3), (1, 1), (1, 2), (1, 3), (2, 2), (2, 3), (3, 3))
+SECOND = ((1, 4), (2, 4), (3, 4), (4, 4))
+BASES = (0, 320)
+SHARES = (16, 8)
+OWNERS = (20, 16)
 F32 = jnp.float32
 BF16 = jnp.bfloat16
 
@@ -44,13 +48,13 @@
 
 
 def krylov_kernel(
-    nb, ng, planes, wy, slots, nproj, owners,
+    nb, ng, planes, wy, slots, nproj,
     x_hbm, p_hbm, pot_hbm, cells_hbm, proj_hbm, scale_hbm, prior_hbm,
-    small_ref, q_ref,
+    a_ref, b_ref, q_ref,
     x_ref, p_ref, pot_ref, cells_ref, proj_ref, scale_ref, prior_ref, in_sems,
     s_ref, g_ref, whole, co, mat, mine, got, out_send, out_recv,
     ext, fin, dens_h, dens_l, prev_h, prev_l, prev_cells, prev_proj,
-    csend, cprev, gpart, grecv, gown,
+    csend, cprev, gpart, grecv_a, grecv_b, gown_a, gown_b,
     halo_send, halo_recv, meta_send, meta_recv, c_send, c_recv,
     band_send, band_recv, rs_send, rs_recv, ag_send, ag_recv,
 ):
@@ -294,95 +298,120 @@
     apply(2, store_to(fin.at[1], 0))
     start_band(4)
 
-    for b in range(BLOCKS):
-        for d in range(1, nb):
-            band_copy(b, d).wait_recv()
+    grecv, gown = (grecv_a, grecv_b), (gown_a, gown_b)
+
+    def piece(s, t):
+        index = (OWNERS[s] * t) // ndev
+        return pl.ds(pl.multiple_of(BASES[s] + index * SHARES[s], 8), SHARES[s])
+
+    def slot(s, t):
+        return s * OWNERS[0] + (OWNERS[s] * t) // ndev
+
+    def owner(s, t):
+        return lax.rem(OWNERS[s] * t, ndev) < OWNERS[s]
+
+    def device(t):
+        return (t // ng, lax.rem(t, ng))
+
+    def rs_copy(s, d):
+        t = lax.rem(me + d, ndev)
+        return t, pltpu.make_async_remote_copy(
+            gpart.at[piece(s, t)], grecv[s].at[d - 1],
+            rs_send.at[slot(s, t)], rs_recv.at[s, d - 1], device(t), MESH)
+
+    def ag_copy(s, d, source):
+        t = lax.rem(me + d, ndev)
+        return pltpu.make_async_remote_copy(
+            gown[s], g_ref.at[piece(s, source)],
+            ag_send.at[s, d - 1], ag_recv.at[slot(s, source)], device(t), MESH)
+
+    def scatter(s):
+        def start(d, carry):
+            t, copy = rs_copy(s, d)
+
+            @pl.when(owner(s, t))
+            def _():
+                copy.start()
+
+            return carry
+
+        lax.fori_loop(1, ndev, start, 0)
+
+    def add_up(s):
+        @pl.when(owner(s, me))
+        def _():
+            def add(d, acc):
+                rs_copy(s, d)[1].wait_recv()
+                return acc + grecv[s][d - 1]
+
+            summed = lax.fori_loop(1, ndev, add, gpart[piece(s, me), :])
+            gown[s][...] = summed
+            g_ref[piece(s, me), :] = summed
+
+            def start(d, carry):
+                ag_copy(s, d, me).start()
+                return carry
+
+            lax.fori_loop(1, ndev, start, 0)
+
+    def collect(s, pairs):
+        def arrive(d, carry):
+            source = lax.rem(me + ndev - d, ndev)
+
+            @pl.when(owner(s, source))
+            def _():
+                ag_copy(s, d, source).wait_recv()
+
+            return carry
+
+        lax.fori_loop(1, ndev, arrive, 0)
+        inverse_total = 1.0 / (lines * ng * wz)
+        for n, (i, j) in enumerate(pairs):
+            top, side = BASES[s] + NB * (n // 2), NB * (n % 2)
+            block = g_ref[top : top + NB, side : side + NB] * inverse_total
+            whole[NB * i : NB * i + NB, NB * j : NB * j + NB] = block
+            if i != j:
+                whole[NB * j : NB * j + NB, NB * i : NB * i + NB] = block.T
 
     many = 4 if part % 4 == 0 else 1
 
-    def gram(i, carry):
-        value = jnp.concatenate(
+    def stacked(i, first):
+        return jnp.concatenate(
             [
-                jnp.concatenate([s_ref[b, many * i + u] for b in range(BLOCKS)], axis=0)
+                jnp.concatenate([s_ref[b, many * i + u] for b in range(first, first + 4)], axis=0)
                 for u in range(many)
             ],
             axis=1,
         )
-        high, low = split(value)
+
+    def gram_first(i, carry):
+        high, low = split(stacked(i, 0))
         return carry + dot_nt(high, high) + dot_nt(high, low) + dot_nt(low, high)
 
-    total = lax.fori_loop(
-        0, part // many, gram, jnp.zeros((BLOCKS * NB, BLOCKS * NB), F32))
-    for n, (i, j) in enumerate(PAIRS):
-        gpart[NB * (n // 2) : NB * (n // 2) + NB, NB * (n % 2) : NB * (n % 2) + NB] = total[
-            NB * i : NB * i + NB, NB * j : NB * j + NB]
-    gpart[NB * 7 :, NB:] = jnp.zeros((NB, NB), F32)
-
-    share = gpart.shape[0] // owners
-
-    def piece(index):
-        return pl.ds(pl.multiple_of(index * share, share), share)
-
-    def device(t):
-        return (t // ng, lax.rem(t, ng))
-
-    def rs_copy(d):
-        t = lax.rem(me + d, ndev)
-        return t, pltpu.make_async_remote_copy(
-            gpart.at[piece(jnp.minimum(t, owners - 1))], grecv.at[d - 1],
-            rs_send.at[d - 1], rs_recv.at[d - 1], device(t), MESH)
-
-    def ag_copy(d, source):
-        t = lax.rem(me + d, ndev)
-        mine = piece(jnp.minimum(source, owners - 1))
-        return pltpu.make_async_remote_copy(
-            gown, g_ref.at[mine], ag_send.at[d - 1], ag_recv.at[d - 1], device(t), MESH)
-
-    def guard(cond, body):
-        if owners == ndev:
-            body()
-        else:
-            pl.when(cond)(body)
-
-    def rs_start(d, carry):
-        t, copy = rs_copy(d)
-        guard(t < owners, lambda: copy.start())
-        return carry
-
-    lax.fori_loop(1, ndev, rs_start, 0)
-
-    def own_sum():
-        def add(d, acc):
-            _, copy = rs_copy(d)
-            copy.wait_recv()
-            return acc + grecv[d - 1]
-
-        summed = lax.fori_loop(1, ndev, add, gpart[piece(jnp.minimum(me, owners - 1)), :])
-        gown[...] = summed
-        g_ref[piece(jnp.minimum(me, owners - 1)), :] = summed
-
-        def ag_start(d, carry):
-            ag_copy(d, me).start()
-            return carry
-
-        lax.fori_loop(1, ndev, ag_start, 0)
-
-    guard(me < owners, own_sum)
-
-    def ag_wait(d, carry):
-        source = lax.rem(me + ndev - d, ndev)
-        guard(source < owners, lambda: ag_copy(d, source).wait_recv())
-        return carry
-
-    lax.fori_loop(1, ndev, ag_wait, 0)
-
-    inverse_total = 1.0 / (lines * ng * wz)
-    for n, (i, j) in enumerate(PAIRS):
-        block = g_ref[NB * (n // 2) : NB * (n // 2) + NB, NB * (n % 2) : NB * (n % 2) + NB]
-        block = block * inverse_total
-        whole[NB * i : NB * i + NB, NB * j : NB * j + NB] = block
-        if i != j:
-            whole[NB * j : NB * j + NB, NB * i : NB * i + NB] = block.T
+    def gram_second(i, carry):
+        high, low = split(stacked(i, 1))
+        return (
+            carry + dot_nt(high, high[3 * NB :]) + dot_nt(high, low[3 * NB :])
+            + dot_nt(low, high[3 * NB :]))
+
+    for b in range(BLOCKS - 1):
+        for d in range(1, nb):
+            band_copy(b, d).wait_recv()
+    total = lax.fori_loop(0, part // many, gram_first, jnp.zeros((4 * NB, 4 * NB), F32))
+    for n, (i, j) in enumerate(FIRST):
+        top, side = NB * (n // 2), NB * (n % 2)
+        gpart[top : top + NB, side : side + NB] = total[NB * i : NB * i + NB, NB * j : NB * j + NB]
+    scatter(0)
+    for d in range(1, nb):
+        band_copy(BLOCKS - 1, d).wait_recv()
+    total = lax.fori_loop(0, part // many, gram_second, jnp.zeros((4 * NB, NB), F32))
+    for n in range(4):
+        top, side = BASES[1] + NB * (n // 2), NB * (n % 2)
+        gpart[top : top + NB, side : side + NB] = total[NB * n : NB * n + NB, :]
+    scatter(1)
+    add_up(0)
+    add_up(1)
+    collect(0, FIRST)
 
     def full_nn(a, b):
         return lax.dot_general(
@@ -411,6 +440,10 @@
     w0 = co[:, 0 : 3 * NB]
     upper1, inverse1 = factor(full_nt(full_nn(w0, whole[0 : 3 * NB, 0 : 3 * NB]), w0))
     q1 = full_nn(inverse1, w0)
+    collect(1, SECOND)
+    corner = whole[2 * NB : 3 * NB, 2 * NB : 3 * NB]
+    whole[0:NB, 4 * NB :] = corner
+    whole[4 * NB :, 0:NB] = corner
     half = full_nn(q1, whole[0 : 3 * NB, 2 * NB : 5 * NB])
     a1 = full_nt(half, q1)
     past = full_nn(full_nt(q1, half), q1)
@@ -423,25 +456,25 @@
     q2 = full_nn(inverse2, w1)
 
     c_high, c_low = split(q2)
-    many = 2 if part % 2 == 0 else 1
+    pair = 2 if part % 2 == 0 else 1
 
     def combine(i, carry):
         value = jnp.concatenate(
             [
-                jnp.concatenate([s_ref[b, many * i + u] for b in range(BLOCKS)], axis=0)
-                for u in range(many)
+                jnp.concatenate([s_ref[b, pair * i + u] for b in range(BLOCKS)], axis=0)
+                for u in range(pair)
             ],
             axis=1,
         )
         v_h, v_l = split(value)
         made = dot_nn(c_high, v_h) + dot_nn(c_low, v_h) + dot_nn(c_high, v_l)
         for t in range(nb):
-            for u in range(many):
-                mine[t, many * i + u] = made[
+            for u in range(pair):
+                mine[t, pair * i + u] = made[
                     t * states : (t + 1) * states, u * wz : (u + 1) * wz]
         return carry
 
-    lax.fori_loop(0, part // many, combine, 0, unroll=2 if part // many > 1 else 1)
+    lax.fori_loop(0, part // pair, combine, 0, unroll=2 if part // pair > 1 else 1)
 
     def out_copy(d):
         t = lax.rem(band + d, nb)
@@ -460,16 +493,25 @@
 
     put(band, mine.at[band])
     pick = jnp.where(
-        lax.broadcasted_iota(jnp.int32, (NB, states), 0)
-        == lax.broadcasted_iota(jnp.int32, (NB, states), 1) + band * states, 1.0, 0.0).astype(F32)
+        lax.broadcasted_iota(jnp.int32, (states, NB), 1)
+        == lax.broadcasted_iota(jnp.int32, (states, NB), 0) + band * states, 1.0, 0.0).astype(F32)
     outs = (a0 + SHIFT * identity, a1 + SHIFT * identity, upper1, upper2)
     for n, value in enumerate(outs):
-        small_ref[n] = full_nn(value, pick)
+        small = (a_ref, b_ref)[n // STEPS]
+        small[n % STEPS] = full_nt(pick, value)
 
     def drain(d, carry):
-        t, copy = rs_copy(d)
-        guard(t < owners, lambda: copy.wait_send())
-        guard(me < owners, lambda: ag_copy(d, me).wait_send())
+        for s in range(2):
+            t, copy = rs_copy(s, d)
+
+            @pl.when(owner(s, t))
+            def _():
+                copy.wait_send()
+
+            @pl.when(owner(s, me))
+            def _():
+                ag_copy(s, d, me).wait_send()
+
         return carry
 
     lax.fori_loop(1, ndev, drain, 0)
@@ -546,21 +588,20 @@
     edge = HALO * wy
     part = lines // nb
     rows = slots * nproj
-    owners = min(ndev, 64)
     live = (jnp.arange(slots, dtype=jnp.int32) < atom_count[0]).astype(F32)
     scale = (atom_strength * live[:, None]).reshape(1, rows)
     dma = pltpu.SemaphoreType.DMA
     vmem = pl.BlockSpec(memory_space=pltpu.VMEM)
-    grows = NB * 8
-    share = grows // owners
-    small, final = pl.pallas_call(
-        functools.partial(krylov_kernel, nb, ng, planes, wy, slots, nproj, owners),
+    grows = NB * 7
+    a_rows, b_rows, final = pl.pallas_call(
+        functools.partial(krylov_kernel, nb, ng, planes, wy, slots, nproj),
         out_shape=(
-            jax.ShapeDtypeStruct((2 * STEPS, NB, states), F32),
+            jax.ShapeDtypeStruct((STEPS, states, NB), F32),
+            jax.ShapeDtypeStruct((STEPS, states, NB), F32),
             jax.ShapeDtypeStruct((states * lines, wz), F32),
         ),
         in_specs=[pl.BlockSpec(memory_space=pl.ANY)] * 7,
-        out_specs=(vmem, vmem),
+        out_specs=(vmem, vmem, vmem),
         scratch_shapes=[
             pltpu.VMEM((states * lines, wz), F32),
             pltpu.VMEM((states * lines, wz), F32),
@@ -589,11 +630,13 @@
             pltpu.VMEM((3, states, 128), F32),
             pltpu.VMEM((3, states, 128), F32),
             pltpu.VMEM((grows, 2 * NB), F32),
-            pltpu.VMEM((ndev - 1, share, 2 * NB), F32),
-            pltpu.VMEM((share, 2 * NB), F32),
+            pltpu.VMEM((ndev - 1, SHARES[0], 2 * NB), F32),
+            pltpu.VMEM((ndev - 1, SHARES[1], 2 * NB), F32),
+            pltpu.VMEM((SHARES[0], 2 * NB), F32),
+            pltpu.VMEM((SHARES[1], 2 * NB), F32),
             dma((6,)), dma((6,)), dma((2,)), dma((2,)), dma((3,)), dma((3,)),
             dma((BLOCKS, nb - 1)), dma((BLOCKS, nb - 1)),
-            dma((ndev - 1,)), dma((ndev - 1,)), dma((ndev - 1,)), dma((ndev - 1,)),
+            dma((sum(OWNERS),)), dma((2, ndev - 1)), dma((2, ndev - 1)), dma((sum(OWNERS),)),
         ],
         compiler_params=pltpu.CompilerParams(
             collective_id=0, has_side_effects=True, vmem_limit_bytes=60 * 2**20),
@@ -606,7 +649,7 @@
         scale,
         previous_coupling,
     )
-    return (small[:STEPS], small[STEPS:], final.reshape(start_block.shape))
+    return (a_rows.swapaxes(1, 2), b_rows.swapaxes(1, 2), final.reshape(start_block.shape))
 
 
 def solution(mesh):

time: 91.4 us -> 84.2 us (0.921)
  Pallas kernels: 84.3 us -> 77.3 us
    pallas_call x1, Pallas kernels: 84.3 us -> 77.3 us  [shards(): pl.pallas_call(functools.partial(krylov_kernel, nb, ng, planes, wy, slots...]
    unnamed x5 -> x7, local copies, waits for them, and re-layouts: 3.91 us -> 4.54 us
where the time goes in v3:
time: 84.2 us; the launch traced here: 83.9 us
  Pallas kernels  77.3 us (92%)
  local copies, waits for them, and re-layouts  5.22 us (6%)
  between operations  1.31 us (2%)
    pallas_call x1, Pallas kernels, shards(): pl.pallas_call(functools.partial(krylov_kernel, nb, ng, planes, wy, slots...  77.3 us
    unnamed x7, local copies, waits for them, and re-layouts  4.54 us

profile of v3, /device:TPU:0, one launch (start us, length us, event | category | flops | bytes accessed | tf_op | source)
XLA Modules:
  0.0 83.9 jit_solution(5372653790639572991)
XLA Ops:
  1.3 0.0 copy-start.1
  1.3 0.7 copy-done.1
  2.0 0.1 copy.12
  2.1 0.6 reshape.33.scale_hbm
  2.7 77.3 %shard_map.103 = (f32[2,32,64]{2,1,0:T(8,128)}, f32[2,32,64]{2,1,0:T(8,128)}, f32[1024,128]{1,0:T(8,128)}) custom-call(f32[1024,128]{1,0:T(8,128)} %bitcast.9, f32[1024,128]{1,0:T(8,128)} %bitcast.10, f32[32,128]{1,0:T(8,128)} %bitcast.14, s32[8,128]{1,0:T(8,128)} %cells_hbm.1, f32[32,128]{1,0:T(8,128)} %bitcast.15, f32[1,32]{1,0:T(1,128)} %reshape.33.scale_hbm, ...), custom_call_target="tpu_custom_call" | custom-call | tf_op jit(solution)/shard_map/pallas_call | solution.py:596
  80.0 0.0 copy-start
  80.0 1.4 %copy.17 = f32[2,64,32]{1,2,0:T(8,128)} copy(f32[2,64,32]{1,2,0:T(8,128)} %bitcast.13) | data formatting | bytes 32768
  81.4 0.0 copy-done
  81.4 0.6 copy.18
  82.0 1.9 %copy.19 = f32[32,8,4,128]{3,2,1,0:T(4,128)} copy(f32[32,8,4,128]{3,2,1,0:T(4,128)} %bitcast.11) | data formatting | bytes 1048576
  (2 shorter events, 0.0 us)
Async XLA Ops:
  1.3 0.7 copy-start.1
  80.0 1.4 %copy-start = (f32[2,32,64]{2,1,0:T(8,128)S(1)}, f32[2,32,64]{2,1,0:T(8,128)}, u32[]{:S(2)}) copy-start(f32[2,32,64]{2,1,0:T(8,128)} %get-tuple-element.7) | copy-start | bytes 49156
